TPU v7x, 32 devices: a whole 2x2x4 slice. The times are simulated.
32 devices in a mesh: tm: 4 (over z), gx: 2 (over x), gy: 4 (over y, core).
Axes of the slice: x: 2, y: 2, z: 4, core: 2. Of those that a mesh axis runs over, the one named last changes fastest.
Arguments:
- state_starts: float32 [4, 64, 64, 512], P('tm', None, 'gx', 'gy'), may hold values from -4 to 4, as said below
- diffusivity: float32 [64], replicated, may hold values from 0.3 to 1.2
- wind: float32 [2, 64], replicated, may hold values from -0.6 to 0.6
Outputs:
- segment_ends: float32 [4, 64, 64, 512], P('tm', None, 'gx', 'gy')
Inputs may be any that keep to these rules, and one draw needn't show every extreme that they name: `state_starts`: states of order one.
All inputs are finite; a program needn't handle non-finite values.
Results may differ from a plain program's by a relative error of at most 0.0001.
Values sent between devices are 32-bit elements; how exact they have to be, the bound alone decides.
A program may use at most 64 MiB of HBM per device.

v0:
```python
import jax
import jax.numpy as jnp
from jax import lax
from jax.sharding import PartitionSpec as P

SUB = 4


time_step = 0.2
weights_low = (0.375, 0.125, 0.0, 0.0)
weights_mid = (0.625, 0.875, 0.875, 0.625)
weights_high = (0.0, 0.0, 0.125, 0.375)


def extended_2(array, sides, width):
    for axis, dim in sides:
        devices, length = (lax.axis_size(axis), array.shape[dim])
        up = [(i, (i + 1) % devices) for i in range(devices - 1)]
        down = [(j, i) for i, j in up]
        last = lax.slice_in_dim(array, length - width, length, axis=dim)
        leading = lax.slice_in_dim(array, 0, width, axis=dim)
        before = lax.ppermute(last, axis, up)
        after = lax.ppermute(leading, axis, down)
        array = jnp.concatenate([before, array, after], axis=dim)
    return array


def passed_along(block, axis, distance):
    devices = range(lax.axis_size(axis))
    route = [(i - distance, i) for i in devices if i - distance in devices]
    return lax.ppermute(block, axis, route)


def advance(padded, diffuse, wind_east, wind_north, factor):
    centre = padded[:, 1:-1, 1:-1]
    east = padded[:, 2:, 1:-1]
    west = padded[:, :-2, 1:-1]
    north = padded[:, 1:-1, 2:]
    south = padded[:, 1:-1, :-2]
    laplace = east + west + north + south - 4.0 * centre
    slope = wind_east * (east - west) * 0.5 + wind_north * (north - south) * 0.5
    return centre + time_step * (factor * diffuse * laplace - centre * slope)


def restrict(field):
    levels, rows, cols = field.shape
    return field.reshape(levels, rows // 4, 4, cols // 4, 4).mean(axis=(2, 4))


def prolong(padded):
    levels, rows_ext, cols_ext = padded.shape
    coarse_rows = rows_ext - 2
    coarse_cols = cols_ext - 2
    parts = [
        weights_low[offset] * padded[:, :-2, :]
        + weights_mid[offset] * padded[:, 1:-1, :]
        + weights_high[offset] * padded[:, 2:, :]
        for offset in range(4)
    ]
    along = jnp.stack(parts, axis=2).reshape(levels, 4 * coarse_rows, cols_ext)
    parts = [
        weights_low[offset] * along[:, :, :-2]
        + weights_mid[offset] * along[:, :, 1:-1]
        + weights_high[offset] * along[:, :, 2:]
        for offset in range(4)
    ]
    return jnp.stack(parts, axis=3).reshape(levels, 4 * coarse_rows, 4 * coarse_cols)


def shards(state_starts, diffusivity, wind):
    begin = state_starts[0]
    diffuse = diffusivity[:, None, None]
    wind_east = wind[0][:, None, None]
    wind_north = wind[1][:, None, None]
    levels, width, height = begin.shape
    column = lax.axis_index("gx")
    row_index = lax.axis_index("gy")
    across = lax.axis_size("gx")
    upward = lax.axis_size("gy")
    field = begin
    for substep in range(SUB):
        padded = extended_2(field, (("gx", 1), ("gy", 2)), 1)
        field = advance(padded, diffuse, wind_east, wind_north, 1.0)
    fine_end = field
    coarse_begin = restrict(begin)
    coarse_wide = width // 4
    coarse_high = height // 4
    rows_global = column * coarse_wide - 1 + jnp.arange(coarse_wide + 2 * 1, dtype=jnp.int32)
    cols_global = row_index * coarse_high - 1 + jnp.arange(coarse_high + 2 * 1, dtype=jnp.int32)
    keep_rows = (rows_global >= 0) & (rows_global < coarse_wide * across)
    keep_cols = (cols_global >= 0) & (cols_global < coarse_high * upward)
    both = keep_rows[:, None] & keep_cols[None, :]
    coarse_inside = jnp.where(both, 1.0, 0.0).astype(jnp.float32)[None]

    def extended(coarse):
        wider = extended_2(coarse, (("gx", 1), ("gy", 2)), 2)
        return advance(wider, diffuse, wind_east, wind_north, 0.25) * coarse_inside

    old_image = extended(coarse_begin)

    def padded_change(coarse):
        return extended(coarse) - old_image

    first_segment = lax.axis_index("tm") == 0

    def next_coarse(coarse):
        return restrict(fine_end + prolong(padded_change(coarse)))

    def one_turn(turn_index, coarse):
        passed = passed_along(next_coarse(coarse), "tm", 1)
        return jnp.where(first_segment, coarse, passed)

    coarse_final = lax.fori_loop(0, lax.axis_size("tm") - 1, one_turn, coarse_begin)
    ending = fine_end + prolong(padded_change(coarse_final))
    return ending[None]


def solution(mesh):
    placed = (P("tm", None, "gx", "gy"), P(), P())
    return jax.shard_map(
        shards, mesh=mesh, in_specs=placed, out_specs=P("tm", None, "gx", "gy"), check_vma=False
    )
```

profile of v0, /device:TPU:25, one launch (start us, length us, event | category | flops | bytes accessed | tf_op | source)
XLA Modules:
  0.0 198.8 jit_solution(6262829469509098009)
XLA Ops:
  0.0 1.8 copy.103
  2.6 3.1 %collective-permute-start.21 = (f32[64,2,32]{0,2,1:T(8,128)S(1)}, f32[64,2,32]{0,2,1:T(8,128)S(1)}, u32[]{:S(2)}, u32[]{:S(2)}) collective-permute-start(f32[64,2,32]{0,2,1:T(8,128)S(1)} %get-tuple-element.169), channel_id=1, source_target_pairs={{0,4},{1,5},{2,6},{3,7},{8,12},{9,13},{10,14},{11,15},{16,20},{17,... | collective-permute-start | bytes 49160 | tf_op jit(solution)/shard_map/ppermute | solution.py:22
  7.0 1.9 copy.102
  9.0 4.0 %collective-permute-start.6 = (f32[64,1,128]{0,1,2:T(1,128)S(1)}, f32[64,1,128]{0,1,2:T(1,128)S(1)}, u32[]{:S(2)}, u32[]{:S(2)}) collective-permute-start(f32[64,1,128]{0,1,2:T(1,128)S(1)} %get-tuple-element.153), channel_id=1, source_target_pairs={{0,4},{1,5},{2,6},{3,7},{8,12},{9,13},{10,14},{11,15},{16,20},{17,... | collective-permute-start | bytes 98312 | tf_op jit(solution)/shard_map/ppermute | solution.py:22
  14.3 3.7 %collective-permute-done.5 = f32[64,1,128]{0,1,2:T(1,128)S(1)} collective-permute-done((f32[64,1,128]{0,1,2:T(1,128)S(1)}, f32[64,1,128]{0,1,2:T(1,128)S(1)}, u32[]{:S(2)}, u32[]{:S(2)}) %collective-permute-start.5) | collective-permute-done | bytes 32800 | tf_op jit(solution)/shard_map/ppermute | solution.py:23
  18.0 4.6 %collective-permute-start.7 = (f32[64,34,1]{0,1,2:T(8,128)S(1)}, f32[64,34,1]{0,1,2:T(8,128)S(1)}, u32[]{:S(2)}, u32[]{:S(2)}) collective-permute-start(f32[64,34,1]{0,1,2:T(8,128)S(1)} %get-tuple-element.145), channel_id=1, source_target_pairs={{1,0},{2,1},{3,2},{5,4},{6,5},{7,6},{9,8},{10,9},{11,10},{13,12},{... | collective-permute-start | bytes 26120 | tf_op jit(solution)/shard_map/ppermute | solution.py:23
  22.6 3.0 %collective-permute-start.8 = (f32[64,34,1]{0,1,2:T(8,128)S(1)}, f32[64,34,1]{0,1,2:T(8,128)S(1)}, u32[]{:S(2)}, u32[]{:S(2)}) collective-permute-start(f32[64,34,1]{0,1,2:T(8,128)S(1)} %get-tuple-element.146), channel_id=1, source_target_pairs={{0,1},{1,2},{2,3},{4,5},{5,6},{6,7},{8,9},{9,10},{10,11},{12,13},{... | collective-permute-start | bytes 26120 | tf_op jit(solution)/shard_map/ppermute | solution.py:22
  26.5 3.5 %multiply_add_fusion.5 = f32[64,32,128]{0,1,2:T(8,128)S(1)} fusion(f32[64,32,128]{0,1,2:T(8,128)S(1)} %bitcast.81, f32[64,1,128]{0,1,2:T(1,128)S(1)} %collective-permute-done.5, f32[64,1,128]{0,1,2:T(1,128)S(1)} %collective-permute-done.6, f32[64,34,1]{0,1,2:T(8,128)S(1)} %collective-permute-done.8, f32[64,34,1]{0,1,2:T(8,128)S(1)} %collective-permute-done.7, ...), kind=kLoop, calls=%fused_computation.64 | loop fusion | flops 6291456 | bytes 2180864 | tf_op jit(solution)/shard_map/add | solution.py:42
  33.1 4.3 %collective-permute-done.9 = f32[64,1,128]{0,1,2:T(1,128)S(1)} collective-permute-done((f32[64,1,128]{0,1,2:T(1,128)S(1)}, f32[64,1,128]{0,1,2:T(1,128)S(1)}, u32[]{:S(2)}, u32[]{:S(2)}) %collective-permute-start.9) | collective-permute-done | bytes 32800 | tf_op jit(solution)/shard_map/ppermute | solution.py:23
  37.5 2.4 %collective-permute-start.11 = (f32[64,34,1]{0,1,2:T(8,128)S(1)}, f32[64,34,1]{0,1,2:T(8,128)S(1)}, u32[]{:S(2)}, u32[]{:S(2)}) collective-permute-start(f32[64,34,1]{0,1,2:T(8,128)S(1)} %get-tuple-element.143), channel_id=1, source_target_pairs={{1,0},{2,1},{3,2},{5,4},{6,5},{7,6},{9,8},{10,9},{11,10},{13,12},{... | collective-permute-start | bytes 26120 | tf_op jit(solution)/shard_map/ppermute | solution.py:23
  39.8 4.3 %collective-permute-start.12 = (f32[64,34,1]{0,1,2:T(8,128)S(1)}, f32[64,34,1]{0,1,2:T(8,128)S(1)}, u32[]{:S(2)}, u32[]{:S(2)}) collective-permute-start(f32[64,34,1]{0,1,2:T(8,128)S(1)} %get-tuple-element.144), channel_id=1, source_target_pairs={{0,1},{1,2},{2,3},{4,5},{5,6},{6,7},{8,9},{9,10},{10,11},{12,13},{... | collective-permute-start | bytes 26120 | tf_op jit(solution)/shard_map/ppermute | solution.py:22
  45.0 3.6 %multiply_add_fusion.4 = f32[64,32,128]{0,1,2:T(8,128)S(1)} fusion(f32[64,32,128]{0,1,2:T(8,128)S(1)} %multiply_add_fusion.5, f32[64,1,128]{0,1,2:T(1,128)S(1)} %collective-permute-done.9, f32[64,1,128]{0,1,2:T(1,128)S(1)} %collective-permute-done.10, f32[64,34,1]{0,1,2:T(8,128)S(1)} %collective-permute-done.12, ...), kind=kLoop, calls=%fused_computation.63 | loop fusion | flops 6291456 | bytes 2180864 | tf_op jit(solution)/shard_map/add | solution.py:42
  51.3 3.7 %collective-permute-done.13 = f32[64,1,128]{0,1,2:T(1,128)S(1)} collective-permute-done((f32[64,1,128]{0,1,2:T(1,128)S(1)}, f32[64,1,128]{0,1,2:T(1,128)S(1)}, u32[]{:S(2)}, u32[]{:S(2)}) %collective-permute-start.13) | collective-permute-done | bytes 32800 | tf_op jit(solution)/shard_map/ppermute | solution.py:23
  55.0 1.9 collective-permute-start.15
  56.9 5.6 %collective-permute-start.16 = (f32[64,34,1]{0,1,2:T(8,128)S(1)}, f32[64,34,1]{0,1,2:T(8,128)S(1)}, u32[]{:S(2)}, u32[]{:S(2)}) collective-permute-start(f32[64,34,1]{0,1,2:T(8,128)S(1)} %get-tuple-element.142), channel_id=1, source_target_pairs={{0,1},{1,2},{2,3},{4,5},{5,6},{6,7},{8,9},{9,10},{10,11},{12,13},{... | collective-permute-start | bytes 26120 | tf_op jit(solution)/shard_map/ppermute | solution.py:22
  62.6 2.4 %collective-permute-start.23 = (f32[64,12,2]{0,2,1:T(2,128)S(1)}, f32[64,12,2]{0,2,1:T(2,128)S(1)}, u32[]{:S(2)}, u32[]{:S(2)}) collective-permute-start(f32[64,12,2]{0,2,1:T(2,128)S(1)} %get-tuple-element.165), channel_id=1, source_target_pairs={{0,1},{1,2},{2,3},{4,5},{5,6},{6,7},{8,9},{9,10},{10,11},{12,13},{... | collective-permute-start | bytes 18440 | tf_op jit(solution)/shard_map/ppermute | solution.py:22
  65.0 1.9 collective-permute-start.24
  67.0 3.6 %multiply_add_fusion.3 = f32[64,32,128]{0,1,2:T(8,128)S(1)} fusion(f32[64,32,128]{0,1,2:T(8,128)S(1)} %multiply_add_fusion.4, f32[64,1,128]{0,1,2:T(1,128)S(1)} %collective-permute-done.13, f32[64,1,128]{0,1,2:T(1,128)S(1)} %collective-permute-done.14, f32[64,34,1]{0,1,2:T(8,128)S(1)} %collective-permute-done.16, ...), kind=kLoop, calls=%fused_computation.62 | loop fusion | flops 6291456 | bytes 2180864 | tf_op jit(solution)/shard_map/add | solution.py:42
  73.8 4.1 %collective-permute-done.17 = f32[64,1,128]{0,1,2:T(1,128)S(1)} collective-permute-done((f32[64,1,128]{0,1,2:T(1,128)S(1)}, f32[64,1,128]{0,1,2:T(1,128)S(1)}, u32[]{:S(2)}, u32[]{:S(2)}) %collective-permute-start.17) | collective-permute-done | bytes 32800 | tf_op jit(solution)/shard_map/ppermute | solution.py:23
  77.9 2.4 %collective-permute-start.19 = (f32[64,34,1]{0,1,2:T(8,128)S(1)}, f32[64,34,1]{0,1,2:T(8,128)S(1)}, u32[]{:S(2)}, u32[]{:S(2)}) collective-permute-start(f32[64,34,1]{0,1,2:T(8,128)S(1)} %get-tuple-element.139), channel_id=1, source_target_pairs={{1,0},{2,1},{3,2},{5,4},{6,5},{7,6},{9,8},{10,9},{11,10},{13,12},{... | collective-permute-start | bytes 26120 | tf_op jit(solution)/shard_map/ppermute | solution.py:23
  80.3 3.9 %collective-permute-start.20 = (f32[64,34,1]{0,1,2:T(8,128)S(1)}, f32[64,34,1]{0,1,2:T(8,128)S(1)}, u32[]{:S(2)}, u32[]{:S(2)}) collective-permute-start(f32[64,34,1]{0,1,2:T(8,128)S(1)} %get-tuple-element.140), channel_id=1, source_target_pairs={{0,1},{1,2},{2,3},{4,5},{5,6},{6,7},{8,9},{9,10},{10,11},{12,13},{... | collective-permute-start | bytes 26120 | tf_op jit(solution)/shard_map/ppermute | solution.py:22
  84.9 3.6 %multiply_add_fusion.2 = f32[64,32,128]{0,1,2:T(8,128)S(1)} fusion(f32[64,32,128]{0,1,2:T(8,128)S(1)} %multiply_add_fusion.3, f32[64,1,128]{0,1,2:T(1,128)S(1)} %collective-permute-done.17, f32[64,1,128]{0,1,2:T(1,128)S(1)} %collective-permute-done.18, f32[64,34,1]{0,1,2:T(8,128)S(1)} %collective-permute-done.20, ...), kind=kLoop, calls=%fused_computation.61 | loop fusion | flops 6291456 | bytes 2180864 | tf_op jit(solution)/shard_map/add | solution.py:42
  89.7 82.0 %while.11 = (s32[]{:T(128)}, f32[64,8,32]{0,2,1:T(8,128)S(1)}, pred[]{:T(512)}, f32[64,32,128]{0,2,1:T(8,128)S(1)}, f32[64,1,1]{0,2,1:T(1,128)S(1)}, /*index=5*/...) while((s32[]{:T(128)}, f32[64,8,32]{0,2,1:T(8,128)S(1)}, ...), condition=%wide.region_3.4_spmd.clone, body=%wide.region_1.3_spmd.clone.sunk | while | flops 3354346 | bytes 9704706 | solution.py:113
  92.5 3.3 %collective-permute-done.1 = f32[64,2,32]{0,2,1:T(8,128)S(1)} collective-permute-done((f32[64,2,32]{0,2,1:T(8,128)S(1)}, f32[64,2,32]{0,2,1:T(8,128)S(1)}, u32[]{:S(2)}, u32[]{:S(2)}) %collective-permute-start.1) | collective-permute-done | bytes 16416 | tf_op jit(solution)/shard_map/while/body/eval_jaxpr/ppermute | solution.py:23
  95.7 1.9 collective-permute-start.2
  97.7 5.6 %collective-permute-start.3 = (f32[64,12,2]{0,2,1:T(2,128)S(1)}, f32[64,12,2]{0,2,1:T(2,128)S(1)}, u32[]{:S(2)}, u32[]{:S(2)}) collective-permute-start(f32[64,12,2]{0,2,1:T(2,128)S(1)} %get-tuple-element.251), channel_id=1, source_target_pairs={{0,1},{1,2},{2,3},{4,5},{5,6},{6,7},{8,9},{9,10},{10,11},{12,13},{... | collective-permute-start | bytes 18440 | tf_op jit(solution)/shard_map/while/body/eval_jaxpr/ppermute | solution.py:22
  107.4 3.1 %fusion.17 = f32[64,8,32]{0,2,1:T(8,128)S(1)} fusion(f32[64,8,4,32,4]{0,4,3,2,1:T(4,128)S(1)} %bitcast.74, f32[64,8,4,32,1]{0,4,3,2,1:T(1,128)S(1)} %copy.125, f32[64,8,4,32,1]{0,4,3,2,1:T(1,128)S(1)} %copy.126, f32[64,8,4,32,1]{0,4,3,2,1:T(1,128)S(1)} %copy.127, f32[64,8,4,32,1]{0,4,3,2,1:T(1,128)S(1)} %copy.128), kind=kLoop, calls=%fused_computation.2.clone.1 | loop fusion | flops 1294336 | bytes 2162688 | tf_op jit(solution)/shard_map/while/body/eval_jaxpr/reduce_sum | solution.py:47
  111.8 4.4 %collective-permute-done.4 = f32[64,8,32]{0,2,1:T(8,128)S(1)} collective-permute-done((f32[64,8,32]{0,2,1:T(8,128)S(1)}, f32[64,8,32]{0,2,1:T(8,128)S(1)}, u32[]{:S(2)}, u32[]{:S(2)}) %collective-permute-start.4) | collective-permute-done | bytes 65568 | tf_op jit(solution)/shard_map/while/body/eval_jaxpr/ppermute | solution.py:31
  116.3 1.3 collective-permute-start
  119.0 3.3 %collective-permute-done.1 = f32[64,2,32]{0,2,1:T(8,128)S(1)} collective-permute-done((f32[64,2,32]{0,2,1:T(8,128)S(1)}, f32[64,2,32]{0,2,1:T(8,128)S(1)}, u32[]{:S(2)}, u32[]{:S(2)}) %collective-permute-start.1) | collective-permute-done | bytes 16416 | tf_op jit(solution)/shard_map/while/body/eval_jaxpr/ppermute | solution.py:23
  122.3 1.9 collective-permute-start.2
  124.2 6.8 %collective-permute-start.3 = (f32[64,12,2]{0,2,1:T(2,128)S(1)}, f32[64,12,2]{0,2,1:T(2,128)S(1)}, u32[]{:S(2)}, u32[]{:S(2)}) collective-permute-start(f32[64,12,2]{0,2,1:T(2,128)S(1)} %get-tuple-element.251), channel_id=1, source_target_pairs={{0,1},{1,2},{2,3},{4,5},{5,6},{6,7},{8,9},{9,10},{10,11},{12,13},{... | collective-permute-start | bytes 18440 | tf_op jit(solution)/shard_map/while/body/eval_jaxpr/ppermute | solution.py:22
  135.1 3.1 %fusion.17 = f32[64,8,32]{0,2,1:T(8,128)S(1)} fusion(f32[64,8,4,32,4]{0,4,3,2,1:T(4,128)S(1)} %bitcast.74, f32[64,8,4,32,1]{0,4,3,2,1:T(1,128)S(1)} %copy.125, f32[64,8,4,32,1]{0,4,3,2,1:T(1,128)S(1)} %copy.126, f32[64,8,4,32,1]{0,4,3,2,1:T(1,128)S(1)} %copy.127, f32[64,8,4,32,1]{0,4,3,2,1:T(1,128)S(1)} %copy.128), kind=kLoop, calls=%fused_computation.2.clone.1 | loop fusion | flops 1294336 | bytes 2162688 | tf_op jit(solution)/shard_map/while/body/eval_jaxpr/reduce_sum | solution.py:47
  139.5 4.4 %collective-permute-done.4 = f32[64,8,32]{0,2,1:T(8,128)S(1)} collective-permute-done((f32[64,8,32]{0,2,1:T(8,128)S(1)}, f32[64,8,32]{0,2,1:T(8,128)S(1)}, u32[]{:S(2)}, u32[]{:S(2)}) %collective-permute-start.4) | collective-permute-done | bytes 65568 | tf_op jit(solution)/shard_map/while/body/eval_jaxpr/ppermute | solution.py:31
  144.0 1.3 collective-permute-start
  146.8 3.3 %collective-permute-done.1 = f32[64,2,32]{0,2,1:T(8,128)S(1)} collective-permute-done((f32[64,2,32]{0,2,1:T(8,128)S(1)}, f32[64,2,32]{0,2,1:T(8,128)S(1)}, u32[]{:S(2)}, u32[]{:S(2)}) %collective-permute-start.1) | collective-permute-done | bytes 16416 | tf_op jit(solution)/shard_map/while/body/eval_jaxpr/ppermute | solution.py:23
  150.0 1.9 collective-permute-start.2
  152.0 6.8 %collective-permute-start.3 = (f32[64,12,2]{0,2,1:T(2,128)S(1)}, f32[64,12,2]{0,2,1:T(2,128)S(1)}, u32[]{:S(2)}, u32[]{:S(2)}) collective-permute-start(f32[64,12,2]{0,2,1:T(2,128)S(1)} %get-tuple-element.251), channel_id=1, source_target_pairs={{0,1},{1,2},{2,3},{4,5},{5,6},{6,7},{8,9},{9,10},{10,11},{12,13},{... | collective-permute-start | bytes 18440 | tf_op jit(solution)/shard_map/while/body/eval_jaxpr/ppermute | solution.py:22
  162.8 3.1 %fusion.17 = f32[64,8,32]{0,2,1:T(8,128)S(1)} fusion(f32[64,8,4,32,4]{0,4,3,2,1:T(4,128)S(1)} %bitcast.74, f32[64,8,4,32,1]{0,4,3,2,1:T(1,128)S(1)} %copy.125, f32[64,8,4,32,1]{0,4,3,2,1:T(1,128)S(1)} %copy.126, f32[64,8,4,32,1]{0,4,3,2,1:T(1,128)S(1)} %copy.127, f32[64,8,4,32,1]{0,4,3,2,1:T(1,128)S(1)} %copy.128), kind=kLoop, calls=%fused_computation.2.clone.1 | loop fusion | flops 1294336 | bytes 2162688 | tf_op jit(solution)/shard_map/while/body/eval_jaxpr/reduce_sum | solution.py:47
  167.2 4.4 %collective-permute-done.4 = f32[64,8,32]{0,2,1:T(8,128)S(1)} collective-permute-done((f32[64,8,32]{0,2,1:T(8,128)S(1)}, f32[64,8,32]{0,2,1:T(8,128)S(1)}, u32[]{:S(2)}, u32[]{:S(2)}) %collective-permute-start.4) | collective-permute-done | bytes 65568 | tf_op jit(solution)/shard_map/while/body/eval_jaxpr/ppermute | solution.py:31
  171.7 1.3 collective-permute-start.25
  174.4 3.3 %collective-permute-done.26 = f32[64,2,32]{0,2,1:T(8,128)S(1)} collective-permute-done((f32[64,2,32]{0,2,1:T(8,128)S(1)}, f32[64,2,32]{0,2,1:T(8,128)S(1)}, u32[]{:S(2)}, u32[]{:S(2)}) %collective-permute-start.26) | collective-permute-done | bytes 16416 | tf_op jit(solution)/shard_map/ppermute | solution.py:23
  177.7 6.8 %collective-permute-start.27 = (f32[64,12,2]{0,2,1:T(2,128)S(1)}, f32[64,12,2]{0,2,1:T(2,128)S(1)}, u32[]{:S(2)}, u32[]{:S(2)}) collective-permute-start(f32[64,12,2]{0,2,1:T(2,128)S(1)} %get-tuple-element.163), channel_id=1, source_target_pairs={{0,1},{1,2},{2,3},{4,5},{5,6},{6,7},{8,9},{9,10},{10,11},{12,13},{... | collective-permute-start | bytes 18440 | tf_op jit(solution)/shard_map/ppermute | solution.py:22
  184.5 2.1 %collective-permute-start.28 = (f32[64,12,2]{0,2,1:T(2,128)S(1)}, f32[64,12,2]{0,2,1:T(2,128)S(1)}, u32[]{:S(2)}, u32[]{:S(2)}) collective-permute-start(f32[64,12,2]{0,2,1:T(2,128)S(1)} %get-tuple-element.164), channel_id=1, source_target_pairs={{1,0},{2,1},{3,2},{5,4},{6,5},{7,6},{9,8},{10,9},{11,10},{13,12},{... | collective-permute-start | bytes 18440 | tf_op jit(solution)/shard_map/ppermute | solution.py:23
  186.7 2.9 %collective-permute-done.28 = f32[64,12,2]{0,2,1:T(2,128)S(1)} collective-permute-done((f32[64,12,2]{0,2,1:T(2,128)S(1)}, f32[64,12,2]{0,2,1:T(2,128)S(1)}, u32[]{:S(2)}, u32[]{:S(2)}) %collective-permute-start.28) | collective-permute-done | bytes 6176 | tf_op jit(solution)/shard_map/ppermute | solution.py:23
  191.0 1.4 copy-done.1
  192.4 3.8 %bitcast_add_fusion = f32[64,32,128]{0,1,2:T(8,128)S(1)} fusion(f32[64,32,32,4]{0,1,3,2:T(8,128)S(1)} %copy.108, f32[64,32,128]{0,1,2:T(8,128)S(1)} %copy-done.1, f32[64]{0:T(128)S(1)} %get-tuple-element.173, f32[64]{0:T(128)S(1)} %get-tuple-element.174, f32[64,1,128]{0,1,2:T(1,128)S(1)} %collective-permute-done.17, ...), kind=kLoop, calls=%fused_computation.60 | loop fusion | flops 6553600 | bytes 3229440 | tf_op jit(solution)/shard_map/add | solution.py:114
  196.2 2.5 %copy.109 = f32[1,64,32,128]{3,2,1,0:T(8,128)} copy(f32[1,64,32,128]{1,2,3,0:T(8,128)S(1)} %bitcast.83) | data formatting | bytes 2097152 | tf_op jit(solution)/shard_map/broadcast_in_dim | solution.py:115
  (142 shorter events, 40.2 us)
Async XLA Ops:
  1.9 5.2 %copy-start.2 = (f32[1,64,32,128]{3,2,1,0:T(8,128)S(1)}, f32[1,64,32,128]{3,2,1,0:T(8,128)}, u32[]{:S(2)}) copy-start(f32[1,64,32,128]{3,2,1,0:T(8,128)} %param.5) | copy-start | bytes 3145732
  2.5 11.8 %copy-start.4 = (f32[2,64]{1,0:T(2,128)S(1)}, f32[2,64]{1,0:T(2,128)}, u32[]{:S(2)}) copy-start(f32[2,64]{1,0:T(2,128)} %param.7) | copy-start | bytes 1540
  2.6 60.0 %collective-permute-start.21 = (f32[64,2,32]{0,2,1:T(8,128)S(1)}, f32[64,2,32]{0,2,1:T(8,128)S(1)}, u32[]{:S(2)}, u32[]{:S(2)}) collective-permute-start(f32[64,2,32]{0,2,1:T(8,128)S(1)} %get-tuple-element.169), channel_id=1, source_target_pairs={{0,4},{1,5},{2,6},{3,7},{8,12},{9,13},{10,14},{11,15},{16,20},{17,... | collective-permute-start | bytes 49160 | tf_op jit(solution)/shard_map/ppermute | solution.py:22
  5.7 20.8 %copy-start.3 = (f32[64]{0:T(128)S(1)}, f32[64]{0:T(128)}, u32[]{:S(2)}) copy-start(f32[64]{0:T(128)} %param.6) | copy-start | bytes 772
  5.7 56.9 %collective-permute-start.22 = (f32[64,2,32]{0,2,1:T(8,128)S(1)}, f32[64,2,32]{0,2,1:T(8,128)S(1)}, u32[]{:S(2)}, u32[]{:S(2)}) collective-permute-start(f32[64,2,32]{0,2,1:T(8,128)S(1)} %get-tuple-element.170), channel_id=1, source_target_pairs={{4,0},{5,1},{6,2},{7,3},{12,8},{13,9},{14,10},{15,11},{20,16},{21,... | collective-permute-start | bytes 49160 | tf_op jit(solution)/shard_map/ppermute | solution.py:23
  9.0 5.3 %collective-permute-start.6 = (f32[64,1,128]{0,1,2:T(1,128)S(1)}, f32[64,1,128]{0,1,2:T(1,128)S(1)}, u32[]{:S(2)}, u32[]{:S(2)}) collective-permute-start(f32[64,1,128]{0,1,2:T(1,128)S(1)} %get-tuple-element.153), channel_id=1, source_target_pairs={{0,4},{1,5},{2,6},{3,7},{8,12},{9,13},{10,14},{11,15},{16,20},{17,... | collective-permute-start | bytes 98312 | tf_op jit(solution)/shard_map/ppermute | solution.py:22
  13.0 5.0 %collective-permute-start.5 = (f32[64,1,128]{0,1,2:T(1,128)S(1)}, f32[64,1,128]{0,1,2:T(1,128)S(1)}, u32[]{:S(2)}, u32[]{:S(2)}) collective-permute-start(f32[64,1,128]{0,1,2:T(1,128)S(1)} %get-tuple-element.154), channel_id=1, source_target_pairs={{4,0},{5,1},{6,2},{7,3},{12,8},{13,9},{14,10},{15,11},{20,16},{21,... | collective-permute-start | bytes 98312 | tf_op jit(solution)/shard_map/ppermute | solution.py:23
  18.0 7.7 %collective-permute-start.7 = (f32[64,34,1]{0,1,2:T(8,128)S(1)}, f32[64,34,1]{0,1,2:T(8,128)S(1)}, u32[]{:S(2)}, u32[]{:S(2)}) collective-permute-start(f32[64,34,1]{0,1,2:T(8,128)S(1)} %get-tuple-element.145), channel_id=1, source_target_pairs={{1,0},{2,1},{3,2},{5,4},{6,5},{7,6},{9,8},{10,9},{11,10},{13,12},{... | collective-permute-start | bytes 26120 | tf_op jit(solution)/shard_map/ppermute | solution.py:23
  22.6 3.9 %collective-permute-start.8 = (f32[64,34,1]{0,1,2:T(8,128)S(1)}, f32[64,34,1]{0,1,2:T(8,128)S(1)}, u32[]{:S(2)}, u32[]{:S(2)}) collective-permute-start(f32[64,34,1]{0,1,2:T(8,128)S(1)} %get-tuple-element.146), channel_id=1, source_target_pairs={{0,1},{1,2},{2,3},{4,5},{5,6},{6,7},{8,9},{9,10},{10,11},{12,13},{... | collective-permute-start | bytes 26120 | tf_op jit(solution)/shard_map/ppermute | solution.py:22
  30.2 3.0 %collective-permute-start.10 = (f32[64,1,128]{0,1,2:T(1,128)S(1)}, f32[64,1,128]{0,1,2:T(1,128)S(1)}, u32[]{:S(2)}, u32[]{:S(2)}) collective-permute-start(f32[64,1,128]{0,1,2:T(1,128)S(1)} %get-tuple-element.151), channel_id=1, source_target_pairs={{0,4},{1,5},{2,6},{3,7},{8,12},{9,13},{10,14},{11,15},{16,20},{17,... | collective-permute-start | bytes 98312 | tf_op jit(solution)/shard_map/ppermute | solution.py:22
  31.5 6.0 %collective-permute-start.9 = (f32[64,1,128]{0,1,2:T(1,128)S(1)}, f32[64,1,128]{0,1,2:T(1,128)S(1)}, u32[]{:S(2)}, u32[]{:S(2)}) collective-permute-start(f32[64,1,128]{0,1,2:T(1,128)S(1)} %get-tuple-element.152), channel_id=1, source_target_pairs={{4,0},{5,1},{6,2},{7,3},{12,8},{13,9},{14,10},{15,11},{20,16},{21,... | collective-permute-start | bytes 98312 | tf_op jit(solution)/shard_map/ppermute | solution.py:23
  37.5 6.7 %collective-permute-start.11 = (f32[64,34,1]{0,1,2:T(8,128)S(1)}, f32[64,34,1]{0,1,2:T(8,128)S(1)}, u32[]{:S(2)}, u32[]{:S(2)}) collective-permute-start(f32[64,34,1]{0,1,2:T(8,128)S(1)} %get-tuple-element.143), channel_id=1, source_target_pairs={{1,0},{2,1},{3,2},{5,4},{6,5},{7,6},{9,8},{10,9},{11,10},{13,12},{... | collective-permute-start | bytes 26120 | tf_op jit(solution)/shard_map/ppermute | solution.py:23
  39.8 5.2 %collective-permute-start.12 = (f32[64,34,1]{0,1,2:T(8,128)S(1)}, f32[64,34,1]{0,1,2:T(8,128)S(1)}, u32[]{:S(2)}, u32[]{:S(2)}) collective-permute-start(f32[64,34,1]{0,1,2:T(8,128)S(1)} %get-tuple-element.144), channel_id=1, source_target_pairs={{0,1},{1,2},{2,3},{4,5},{5,6},{6,7},{8,9},{9,10},{10,11},{12,13},{... | collective-permute-start | bytes 26120 | tf_op jit(solution)/shard_map/ppermute | solution.py:22
  48.7 2.6 %collective-permute-start.14 = (f32[64,1,128]{0,1,2:T(1,128)S(1)}, f32[64,1,128]{0,1,2:T(1,128)S(1)}, u32[]{:S(2)}, u32[]{:S(2)}) collective-permute-start(f32[64,1,128]{0,1,2:T(1,128)S(1)} %get-tuple-element.149), channel_id=1, source_target_pairs={{0,4},{1,5},{2,6},{3,7},{8,12},{9,13},{10,14},{11,15},{16,20},{17,... | collective-permute-start | bytes 98312 | tf_op jit(solution)/shard_map/ppermute | solution.py:22
  50.0 5.0 %collective-permute-start.13 = (f32[64,1,128]{0,1,2:T(1,128)S(1)}, f32[64,1,128]{0,1,2:T(1,128)S(1)}, u32[]{:S(2)}, u32[]{:S(2)}) collective-permute-start(f32[64,1,128]{0,1,2:T(1,128)S(1)} %get-tuple-element.150), channel_id=1, source_target_pairs={{4,0},{5,1},{6,2},{7,3},{12,8},{13,9},{14,10},{15,11},{20,16},{21,... | collective-permute-start | bytes 98312 | tf_op jit(solution)/shard_map/ppermute | solution.py:23
  55.0 12.0 %collective-permute-start.15 = (f32[64,34,1]{0,1,2:T(8,128)S(1)}, f32[64,34,1]{0,1,2:T(8,128)S(1)}, u32[]{:S(2)}, u32[]{:S(2)}) collective-permute-start(f32[64,34,1]{0,1,2:T(8,128)S(1)} %get-tuple-element.141), channel_id=1, source_target_pairs={{1,0},{2,1},{3,2},{5,4},{6,5},{7,6},{9,8},{10,9},{11,10},{13,12},{... | collective-permute-start | bytes 26120 | tf_op jit(solution)/shard_map/ppermute | solution.py:23
  56.9 10.0 %collective-permute-start.16 = (f32[64,34,1]{0,1,2:T(8,128)S(1)}, f32[64,34,1]{0,1,2:T(8,128)S(1)}, u32[]{:S(2)}, u32[]{:S(2)}) collective-permute-start(f32[64,34,1]{0,1,2:T(8,128)S(1)} %get-tuple-element.142), channel_id=1, source_target_pairs={{0,1},{1,2},{2,3},{4,5},{5,6},{6,7},{8,9},{9,10},{10,11},{12,13},{... | collective-permute-start | bytes 26120 | tf_op jit(solution)/shard_map/ppermute | solution.py:22
  62.6 10.6 %collective-permute-start.23 = (f32[64,12,2]{0,2,1:T(2,128)S(1)}, f32[64,12,2]{0,2,1:T(2,128)S(1)}, u32[]{:S(2)}, u32[]{:S(2)}) collective-permute-start(f32[64,12,2]{0,2,1:T(2,128)S(1)} %get-tuple-element.165), channel_id=1, source_target_pairs={{0,1},{1,2},{2,3},{4,5},{5,6},{6,7},{8,9},{9,10},{10,11},{12,13},{... | collective-permute-start | bytes 18440 | tf_op jit(solution)/shard_map/ppermute | solution.py:22
  65.0 8.2 %collective-permute-start.24 = (f32[64,12,2]{0,2,1:T(2,128)S(1)}, f32[64,12,2]{0,2,1:T(2,128)S(1)}, u32[]{:S(2)}, u32[]{:S(2)}) collective-permute-start(f32[64,12,2]{0,2,1:T(2,128)S(1)} %get-tuple-element.166), channel_id=1, source_target_pairs={{1,0},{2,1},{3,2},{5,4},{6,5},{7,6},{9,8},{10,9},{11,10},{13,12},{... | collective-permute-start | bytes 18440 | tf_op jit(solution)/shard_map/ppermute | solution.py:23
  70.6 17.9 %copy-start = (f32[64,32,128]{0,1,2:T(8,128)}, f32[64,32,128]{0,1,2:T(8,128)S(1)}, u32[]{:S(2)}) copy-start(f32[64,32,128]{0,1,2:T(8,128)S(1)} %multiply_add_fusion.3) | copy-start | bytes 3145732
  70.7 3.1 %collective-permute-start.18 = (f32[64,1,128]{0,1,2:T(1,128)S(1)}, f32[64,1,128]{0,1,2:T(1,128)S(1)}, u32[]{:S(2)}, u32[]{:S(2)}) collective-permute-start(f32[64,1,128]{0,1,2:T(1,128)S(1)} %get-tuple-element.147), channel_id=1, source_target_pairs={{0,4},{1,5},{2,6},{3,7},{8,12},{9,13},{10,14},{11,15},{16,20},{17,... | collective-permute-start | bytes 98312 | tf_op jit(solution)/shard_map/ppermute | solution.py:22
  72.0 5.9 %collective-permute-start.17 = (f32[64,1,128]{0,1,2:T(1,128)S(1)}, f32[64,1,128]{0,1,2:T(1,128)S(1)}, u32[]{:S(2)}, u32[]{:S(2)}) collective-permute-start(f32[64,1,128]{0,1,2:T(1,128)S(1)} %get-tuple-element.148), channel_id=1, source_target_pairs={{4,0},{5,1},{6,2},{7,3},{12,8},{13,9},{14,10},{15,11},{20,16},{21,... | collective-permute-start | bytes 98312 | tf_op jit(solution)/shard_map/ppermute | solution.py:23
  77.9 6.5 %collective-permute-start.19 = (f32[64,34,1]{0,1,2:T(8,128)S(1)}, f32[64,34,1]{0,1,2:T(8,128)S(1)}, u32[]{:S(2)}, u32[]{:S(2)}) collective-permute-start(f32[64,34,1]{0,1,2:T(8,128)S(1)} %get-tuple-element.139), channel_id=1, source_target_pairs={{1,0},{2,1},{3,2},{5,4},{6,5},{7,6},{9,8},{10,9},{11,10},{13,12},{... | collective-permute-start | bytes 26120 | tf_op jit(solution)/shard_map/ppermute | solution.py:23
  80.3 4.6 %collective-permute-start.20 = (f32[64,34,1]{0,1,2:T(8,128)S(1)}, f32[64,34,1]{0,1,2:T(8,128)S(1)}, u32[]{:S(2)}, u32[]{:S(2)}) collective-permute-start(f32[64,34,1]{0,1,2:T(8,128)S(1)} %get-tuple-element.140), channel_id=1, source_target_pairs={{0,1},{1,2},{2,3},{4,5},{5,6},{6,7},{8,9},{9,10},{10,11},{12,13},{... | collective-permute-start | bytes 26120 | tf_op jit(solution)/shard_map/ppermute | solution.py:22
  89.8 2.7 %collective-permute-start = (f32[64,2,32]{0,2,1:T(8,128)S(1)}, f32[64,2,32]{0,2,1:T(8,128)S(1)}, u32[]{:S(2)}, u32[]{:S(2)}) collective-permute-start(f32[64,2,32]{0,2,1:T(8,128)S(1)} %get-tuple-element.248), channel_id=1, source_target_pairs={{0,4},{1,5},{2,6},{3,7},{8,12},{9,13},{10,14},{11,15},{16,20},{17,... | collective-permute-start | bytes 49160 | tf_op jit(solution)/shard_map/while/body/eval_jaxpr/ppermute | solution.py:22
  91.1 4.7 %collective-permute-start.1 = (f32[64,2,32]{0,2,1:T(8,128)S(1)}, f32[64,2,32]{0,2,1:T(8,128)S(1)}, u32[]{:S(2)}, u32[]{:S(2)}) collective-permute-start(f32[64,2,32]{0,2,1:T(8,128)S(1)} %get-tuple-element.249), channel_id=1, source_target_pairs={{4,0},{5,1},{6,2},{7,3},{12,8},{13,9},{14,10},{15,11},{20,16},{21,... | collective-permute-start | bytes 49160 | tf_op jit(solution)/shard_map/while/body/eval_jaxpr/ppermute | solution.py:23
  95.7 7.6 %collective-permute-start.2 = (f32[64,12,2]{0,2,1:T(2,128)S(1)}, f32[64,12,2]{0,2,1:T(2,128)S(1)}, u32[]{:S(2)}, u32[]{:S(2)}) collective-permute-start(f32[64,12,2]{0,2,1:T(2,128)S(1)} %get-tuple-element.250), channel_id=1, source_target_pairs={{1,0},{2,1},{3,2},{5,4},{6,5},{7,6},{9,8},{10,9},{11,10},{13,12},{... | collective-permute-start | bytes 18440 | tf_op jit(solution)/shard_map/while/body/eval_jaxpr/ppermute | solution.py:23
  97.7 6.5 %collective-permute-start.3 = (f32[64,12,2]{0,2,1:T(2,128)S(1)}, f32[64,12,2]{0,2,1:T(2,128)S(1)}, u32[]{:S(2)}, u32[]{:S(2)}) collective-permute-start(f32[64,12,2]{0,2,1:T(2,128)S(1)} %get-tuple-element.251), channel_id=1, source_target_pairs={{0,1},{1,2},{2,3},{4,5},{5,6},{6,7},{8,9},{9,10},{10,11},{12,13},{... | collective-permute-start | bytes 18440 | tf_op jit(solution)/shard_map/while/body/eval_jaxpr/ppermute | solution.py:22
  110.5 5.7 %collective-permute-start.4 = (f32[64,8,32]{0,2,1:T(8,128)S(1)}, f32[64,8,32]{0,2,1:T(8,128)S(1)}, u32[]{:S(2)}, u32[]{:S(2)}) collective-permute-start(f32[64,8,32]{0,2,1:T(8,128)S(1)} %broadcast_multiply_fusion.4), channel_id=1, source_target_pairs={{0,8},{8,16},{16,24},{1,9},{9,17},{17,25},{2,10},{10,18},{18,26},{... | collective-permute-start | bytes 196616 | tf_op jit(solution)/shard_map/while/body/eval_jaxpr/ppermute | solution.py:31
  116.3 2.7 %collective-permute-start = (f32[64,2,32]{0,2,1:T(8,128)S(1)}, f32[64,2,32]{0,2,1:T(8,128)S(1)}, u32[]{:S(2)}, u32[]{:S(2)}) collective-permute-start(f32[64,2,32]{0,2,1:T(8,128)S(1)} %get-tuple-element.248), channel_id=1, source_target_pairs={{0,4},{1,5},{2,6},{3,7},{8,12},{9,13},{10,14},{11,15},{16,20},{17,... | collective-permute-start | bytes 49160 | tf_op jit(solution)/shard_map/while/body/eval_jaxpr/ppermute | solution.py:22
  117.6 4.7 %collective-permute-start.1 = (f32[64,2,32]{0,2,1:T(8,128)S(1)}, f32[64,2,32]{0,2,1:T(8,128)S(1)}, u32[]{:S(2)}, u32[]{:S(2)}) collective-permute-start(f32[64,2,32]{0,2,1:T(8,128)S(1)} %get-tuple-element.249), channel_id=1, source_target_pairs={{4,0},{5,1},{6,2},{7,3},{12,8},{13,9},{14,10},{15,11},{20,16},{21,... | collective-permute-start | bytes 49160 | tf_op jit(solution)/shard_map/while/body/eval_jaxpr/ppermute | solution.py:23
  122.3 8.7 %collective-permute-start.2 = (f32[64,12,2]{0,2,1:T(2,128)S(1)}, f32[64,12,2]{0,2,1:T(2,128)S(1)}, u32[]{:S(2)}, u32[]{:S(2)}) collective-permute-start(f32[64,12,2]{0,2,1:T(2,128)S(1)} %get-tuple-element.250), channel_id=1, source_target_pairs={{1,0},{2,1},{3,2},{5,4},{6,5},{7,6},{9,8},{10,9},{11,10},{13,12},{... | collective-permute-start | bytes 18440 | tf_op jit(solution)/shard_map/while/body/eval_jaxpr/ppermute | solution.py:23
  124.2 7.6 %collective-permute-start.3 = (f32[64,12,2]{0,2,1:T(2,128)S(1)}, f32[64,12,2]{0,2,1:T(2,128)S(1)}, u32[]{:S(2)}, u32[]{:S(2)}) collective-permute-start(f32[64,12,2]{0,2,1:T(2,128)S(1)} %get-tuple-element.251), channel_id=1, source_target_pairs={{0,1},{1,2},{2,3},{4,5},{5,6},{6,7},{8,9},{9,10},{10,11},{12,13},{... | collective-permute-start | bytes 18440 | tf_op jit(solution)/shard_map/while/body/eval_jaxpr/ppermute | solution.py:22
  138.2 5.7 %collective-permute-start.4 = (f32[64,8,32]{0,2,1:T(8,128)S(1)}, f32[64,8,32]{0,2,1:T(8,128)S(1)}, u32[]{:S(2)}, u32[]{:S(2)}) collective-permute-start(f32[64,8,32]{0,2,1:T(8,128)S(1)} %broadcast_multiply_fusion.4), channel_id=1, source_target_pairs={{0,8},{8,16},{16,24},{1,9},{9,17},{17,25},{2,10},{10,18},{18,26},{... | collective-permute-start | bytes 196616 | tf_op jit(solution)/shard_map/while/body/eval_jaxpr/ppermute | solution.py:31
  144.0 2.7 %collective-permute-start = (f32[64,2,32]{0,2,1:T(8,128)S(1)}, f32[64,2,32]{0,2,1:T(8,128)S(1)}, u32[]{:S(2)}, u32[]{:S(2)}) collective-permute-start(f32[64,2,32]{0,2,1:T(8,128)S(1)} %get-tuple-element.248), channel_id=1, source_target_pairs={{0,4},{1,5},{2,6},{3,7},{8,12},{9,13},{10,14},{11,15},{16,20},{17,... | collective-permute-start | bytes 49160 | tf_op jit(solution)/shard_map/while/body/eval_jaxpr/ppermute | solution.py:22
  145.4 4.7 %collective-permute-start.1 = (f32[64,2,32]{0,2,1:T(8,128)S(1)}, f32[64,2,32]{0,2,1:T(8,128)S(1)}, u32[]{:S(2)}, u32[]{:S(2)}) collective-permute-start(f32[64,2,32]{0,2,1:T(8,128)S(1)} %get-tuple-element.249), channel_id=1, source_target_pairs={{4,0},{5,1},{6,2},{7,3},{12,8},{13,9},{14,10},{15,11},{20,16},{21,... | collective-permute-start | bytes 49160 | tf_op jit(solution)/shard_map/while/body/eval_jaxpr/ppermute | solution.py:23
  150.0 8.7 %collective-permute-start.2 = (f32[64,12,2]{0,2,1:T(2,128)S(1)}, f32[64,12,2]{0,2,1:T(2,128)S(1)}, u32[]{:S(2)}, u32[]{:S(2)}) collective-permute-start(f32[64,12,2]{0,2,1:T(2,128)S(1)} %get-tuple-element.250), channel_id=1, source_target_pairs={{1,0},{2,1},{3,2},{5,4},{6,5},{7,6},{9,8},{10,9},{11,10},{13,12},{... | collective-permute-start | bytes 18440 | tf_op jit(solution)/shard_map/while/body/eval_jaxpr/ppermute | solution.py:23
  152.0 7.6 %collective-permute-start.3 = (f32[64,12,2]{0,2,1:T(2,128)S(1)}, f32[64,12,2]{0,2,1:T(2,128)S(1)}, u32[]{:S(2)}, u32[]{:S(2)}) collective-permute-start(f32[64,12,2]{0,2,1:T(2,128)S(1)} %get-tuple-element.251), channel_id=1, source_target_pairs={{0,1},{1,2},{2,3},{4,5},{5,6},{6,7},{8,9},{9,10},{10,11},{12,13},{... | collective-permute-start | bytes 18440 | tf_op jit(solution)/shard_map/while/body/eval_jaxpr/ppermute | solution.py:22
  165.9 5.7 %collective-permute-start.4 = (f32[64,8,32]{0,2,1:T(8,128)S(1)}, f32[64,8,32]{0,2,1:T(8,128)S(1)}, u32[]{:S(2)}, u32[]{:S(2)}) collective-permute-start(f32[64,8,32]{0,2,1:T(8,128)S(1)} %broadcast_multiply_fusion.4), channel_id=1, source_target_pairs={{0,8},{8,16},{16,24},{1,9},{9,17},{17,25},{2,10},{10,18},{18,26},{... | collective-permute-start | bytes 196616 | tf_op jit(solution)/shard_map/while/body/eval_jaxpr/ppermute | solution.py:31
  171.7 2.6 %collective-permute-start.25 = (f32[64,2,32]{0,2,1:T(8,128)S(1)}, f32[64,2,32]{0,2,1:T(8,128)S(1)}, u32[]{:S(2)}, u32[]{:S(2)}) collective-permute-start(f32[64,2,32]{0,2,1:T(8,128)S(1)} %get-tuple-element.168), channel_id=1, source_target_pairs={{0,4},{1,5},{2,6},{3,7},{8,12},{9,13},{10,14},{11,15},{16,20},{17,... | collective-permute-start | bytes 49160 | tf_op jit(solution)/shard_map/ppermute | solution.py:22
  173.1 4.7 %collective-permute-start.26 = (f32[64,2,32]{0,2,1:T(8,128)S(1)}, f32[64,2,32]{0,2,1:T(8,128)S(1)}, u32[]{:S(2)}, u32[]{:S(2)}) collective-permute-start(f32[64,2,32]{0,2,1:T(8,128)S(1)} %get-tuple-element.167), channel_id=1, source_target_pairs={{4,0},{5,1},{6,2},{7,3},{12,8},{13,9},{14,10},{15,11},{20,16},{21,... | collective-permute-start | bytes 49160 | tf_op jit(solution)/shard_map/ppermute | solution.py:23
  177.7 8.9 %collective-permute-start.27 = (f32[64,12,2]{0,2,1:T(2,128)S(1)}, f32[64,12,2]{0,2,1:T(2,128)S(1)}, u32[]{:S(2)}, u32[]{:S(2)}) collective-permute-start(f32[64,12,2]{0,2,1:T(2,128)S(1)} %get-tuple-element.163), channel_id=1, source_target_pairs={{0,1},{1,2},{2,3},{4,5},{5,6},{6,7},{8,9},{9,10},{10,11},{12,13},{... | collective-permute-start | bytes 18440 | tf_op jit(solution)/shard_map/ppermute | solution.py:22
  184.5 5.0 %collective-permute-start.28 = (f32[64,12,2]{0,2,1:T(2,128)S(1)}, f32[64,12,2]{0,2,1:T(2,128)S(1)}, u32[]{:S(2)}, u32[]{:S(2)}) collective-permute-start(f32[64,12,2]{0,2,1:T(2,128)S(1)} %get-tuple-element.164), channel_id=1, source_target_pairs={{1,0},{2,1},{3,2},{5,4},{6,5},{7,6},{9,8},{10,9},{11,10},{13,12},{... | collective-permute-start | bytes 18440 | tf_op jit(solution)/shard_map/ppermute | solution.py:23
  190.8 1.6 copy-start.1
where the time goes:
time: 200 us; the launch traced here: 199 us
  starting transfers between devices  98.1 us (49%)
  waiting for transfers between devices  50.3 us (25%)
  other arithmetic  31.7 us (16%)
  local copies, waits for them, and re-layouts  17.5 us (9%)
    ppermute x18, starting transfers between devices, extended_2(): before = lax.ppermute(last, axis, up)  61.5 us
    ppermute x18, starting transfers between devices, extended_2(): after = lax.ppermute(leading, axis, down)  32.7 us
    ppermute x18, waiting for transfers between devices, extended_2(): after = lax.ppermute(leading, axis, down)  31.7 us
    add x4, other arithmetic, advance(): return centre + time_step * (factor * diffuse * laplace - centre * slope)  14.3 us
    ppermute x3, waiting for transfers between devices, passed_along(): return lax.ppermute(block, axis, route)  13.2 us
    reduce_sum x4, other arithmetic, restrict(): return field.reshape(levels, rows // 4, 4, cols // 4, 4).mean(axis=(2, 4))  9.99 us
    another operation x13, local copies, waits for them, and re-layouts, prolong(): jnp.stack(parts, axis=3).reshape(levels, 4 * coarse_rows, 4 * coarse_cols)  6.66 us
    unnamed x15, local copies, waits for them, and re-layouts  6.36 us
  transfers between devices with their start and end apart: 39, of which 20 were waited for; matrix products, arithmetic and copies ran while one was open for 7% of the time, Pallas kernels for 0%

commit v1 on v0

v1 whole, which is shorter than its diff:
```python
import functools

import jax
import jax.numpy as jnp
from jax import lax
from jax.experimental import pallas as pl
from jax.experimental.pallas import tpu as pltpu
from jax.sharding import PartitionSpec as P

SUB = 4
REACH = SUB
RATIO = 4
LANES = 128
EDGE = 8
FRONT = 2 * EDGE
COARSE_REACH = 2

time_step = 0.2
weights_low = (0.375, 0.125, 0.0, 0.0)
weights_mid = (0.625, 0.875, 0.875, 0.625)
weights_high = (0.0, 0.0, 0.125, 0.375)
mean_side, mean_mid = 0.125, 0.75

PLANE = tuple((dx, dy) for dx in (-1, 0, 1) for dy in (-1, 0, 1))
AROUND = tuple(d for d in PLANE if d != (0, 0))


def conjunction(conditions):
    total = True
    for condition in conditions:
        total = condition if total is True else jnp.logical_and(total, condition)
    return total


def kernel(
    sizes, levels, rows, cols,
    x_ref, diff_ref, wind_ref, out_ref,
    first, second, x_send, x_recv, old_wide, new_wide, extended, old_image, change,
    sent, fine_mean, line, fine_line,
    fine_out, fine_in, old_out, old_in, chain_out, chain_in,
):
    n_tm, n_gx, n_gy = sizes
    tm, gx, gy = lax.axis_index("tm"), lax.axis_index("gx"), lax.axis_index("gy")
    packs = LANES // levels
    part = rows // packs
    part_c = part // RATIO
    cols_c = cols // RATIO
    wide = part + 2 * REACH
    wide_c = part_c + 2 * COARSE_REACH
    end = FRONT + cols
    end_c = FRONT + cols_c

    def there(dz, dx, dy):
        tests = []
        for place, move, count in ((tm, dz, n_tm), (gx, dx, n_gx), (gy, dy, n_gy)):
            if move < 0:
                tests.append(place > 0)
            if move > 0:
                tests.append(place < count - 1)
        return conjunction(tests)

    def guarded(condition, action):
        if condition is True:
            action()
        else:
            pl.when(condition)(action)

    def target(dz, dx, dy):
        return (tm + dz, gx + dx, gy + dy)

    barrier = pltpu.get_barrier_semaphore()
    partners = [(dz, dx, dy) for dz in (-1, 0, 1) for dx, dy in PLANE if (dz, dx, dy) != (0, 0, 0)]
    awaited = jnp.int32(0)
    for move in partners:
        def greet(move=move):
            pl.semaphore_signal(barrier, inc=1, device_id=target(*move), device_id_type=pl.DeviceIdType.MESH)
        guarded(there(*move), greet)
        awaited = awaited + there(*move).astype(jnp.int32)

    def send_all(copies, dz, moves):
        for move in moves:
            guarded(there(dz, *move), lambda move=move: copies[move].start())

    def sends_done(copies, dz, moves):
        for move in moves:
            guarded(there(dz, *move), lambda move=move: copies[move].wait_send())

    def all_arrived(copies, dz, moves):
        for dx, dy in moves:
            guarded(there(-dz, -dx, -dy), lambda move=(dx, dy): copies[move].wait_recv())

    def remote(source, landing, out_sem, in_sem, move):
        return pltpu.make_async_remote_copy(
            src_ref=source, dst_ref=landing, send_sem=out_sem, recv_sem=in_sem,
            device_id=target(*move), device_id_type=pl.DeviceIdType.MESH,
        )

    def index_of(move):
        return (move[0] + 1) * 3 + move[1] + 1

    fine_copies = {}
    for move in AROUND:
        dx, dy = move
        k = index_of(move)
        if dy == 0:
            source, landing = x_send.at[(dx + 1) // 2], x_recv.at[(dx + 1) // 2]
        else:
            take_row, put_row, height = {
                0: (REACH, REACH, part), -1: (REACH, REACH + part, REACH), 1: (part, 0, REACH)
            }[dx]
            take, put = {-1: (FRONT, end), 1: (end - EDGE, FRONT - EDGE)}[dy]
            source = first.at[pl.ds(take_row, height), pl.ds(take, EDGE)]
            landing = first.at[pl.ds(put_row, height), pl.ds(put, EDGE)]
        fine_copies[move] = remote(source, landing, fine_out.at[k], fine_in.at[k], (0, dx, dy))

    def coarse_copies(buffer, row0, col0, landing_buffer, out_sems, in_sems, dz, moves):
        copies = {}
        for move in moves:
            dx, dy = move
            k = index_of(move)
            take_row, put_row, height = {
                0: (0, COARSE_REACH, part_c),
                -1: (0, COARSE_REACH + part_c, COARSE_REACH),
                1: (part_c - COARSE_REACH, 0, COARSE_REACH),
            }[dx]
            take, put, width = {
                0: (0, FRONT, cols_c), -1: (0, end_c, EDGE), 1: (cols_c - EDGE, FRONT - EDGE, EDGE)
            }[dy]
            copies[move] = remote(
                buffer.at[pl.ds(row0 + take_row, height), pl.ds(col0 + take, width)],
                landing_buffer.at[pl.ds(put_row, height), pl.ds(put, width)],
                out_sems.at[k], in_sems.at[k], (dz, dx, dy),
            )
        return copies

    old_copies = coarse_copies(old_wide, COARSE_REACH, FRONT, old_wide, old_out, old_in, 0, AROUND)
    chain_copies = coarse_copies(sent, 0, 0, new_wide, chain_out, chain_in, 1, PLANE)

    lane = lax.broadcasted_iota(jnp.int32, (1, LANES), 1)
    pack = lane // levels

    def packed(row):
        return jnp.concatenate([row] * packs, axis=1)

    diffuse = packed(diff_ref[...])
    east_wind = packed(wind_ref[0:1, :])
    north_wind = packed(wind_ref[1:2, :])

    def constants(factor):
        spread = (time_step * factor) * diffuse
        return 1.0 - 4.0 * spread, spread, (0.5 * time_step) * east_wind, (0.5 * time_step) * north_wind

    fine_constants = constants(1.0)
    coarse_constants = constants(0.25)

    def advance(source, row, start, count, consts):
        keep, spread, along_x, along_y = consts
        centre = source[row, pl.ds(start, count), :]
        east = source[row + 1, pl.ds(start, count), :]
        west = source[row - 1, pl.ds(start, count), :]
        north = source[row, pl.ds(start + 1, count), :]
        south = source[row, pl.ds(start - 1, count), :]
        pushed = along_x * (east - west) + along_y * (north - south)
        return centre * (keep - pushed) + spread * ((east + west) + (north + south))

    def native_row(x):
        if x < 0:
            return x_recv[1, x + REACH]
        if x >= rows:
            return x_recv[0, x - rows]
        return x_ref[pl.ds(x, levels, stride=rows), :]

    def bring_in(row):
        stacked = jnp.concatenate([native_row(p * part + row - REACH) for p in range(packs)], axis=0)
        first[row, pl.ds(FRONT, cols), :] = stacked.T

    for r in range(REACH):
        x_send[0, r] = native_row(r)
        x_send[1, r] = native_row(rows - REACH + r)
    pl.semaphore_wait(barrier, awaited)
    x_moves = tuple(m for m in AROUND if m[1] == 0)
    y_moves = tuple(m for m in AROUND if m[1] != 0)
    send_all(fine_copies, 0, x_moves)
    for row in range(REACH, REACH + part):
        bring_in(row)
    send_all(fine_copies, 0, y_moves)

    def restricted(source, row):
        total = source[REACH + row * RATIO, pl.ds(FRONT, cols), :]
        for r in range(1, RATIO):
            total = total + source[REACH + row * RATIO + r, pl.ds(FRONT, cols), :]
        fine_line[...] = total
        mean = fine_line[pl.ds(0, cols_c, stride=RATIO), :]
        for o in range(1, RATIO):
            mean = mean + fine_line[pl.ds(o, cols_c, stride=RATIO), :]
        return mean * (1.0 / RATIO**2)

    for row in range(part_c):
        old_wide[COARSE_REACH + row, pl.ds(FRONT, cols_c), :] = restricted(first, row)
    send_all(old_copies, 0, AROUND)

    def inside_x(row, reach, length):
        place = (gx * packs + pack) * length + (row - reach)
        return jnp.logical_and(place >= 0, place < n_gx * packs * length)

    def inside_y(start, count, length):
        place = gy * length + (start - FRONT) + lax.broadcasted_iota(jnp.int32, (count, LANES), 0)
        return jnp.logical_and(place >= 0, place < n_gy * length)

    all_arrived(fine_copies, 0, x_moves)
    for row in [*range(REACH), *range(REACH + part, wide)]:
        bring_in(row)
        inner = first[row, pl.ds(FRONT, cols), :]
        first[row, pl.ds(FRONT, cols), :] = jnp.where(inside_x(row, REACH, part), inner, 0.0)
    all_arrived(fine_copies, 0, y_moves)
    sends_done(fine_copies, 0, AROUND)
    low_lanes = lane < levels
    high_lanes = lane >= LANES - levels
    for start in (FRONT - EDGE, end):
        mask_y = inside_y(start, EDGE, cols)
        for row in [*range(REACH), *range(REACH + part, wide), *range(REACH, REACH + part)]:
            here = first[row, pl.ds(start, EDGE), :]
            if row < REACH:
                here = pltpu.roll(jnp.where(high_lanes, here, first[row + part, pl.ds(start, EDGE), :]), levels, 1)
            elif row >= REACH + part:
                here = pltpu.roll(jnp.where(low_lanes, here, first[row - part, pl.ds(start, EDGE), :]), LANES - levels, 1)
            mask = mask_y
            if not REACH <= row < REACH + part:
                mask = jnp.logical_and(mask, inside_x(row, REACH, part))
            first[row, pl.ds(start, EDGE), :] = jnp.where(mask, here, 0.0)

    south_mask = inside_y(FRONT - EDGE, EDGE, cols)
    north_mask = inside_y(end, EDGE, cols)
    half = cols // 2
    source, dest = first, second
    for step in range(1, SUB + 1):
        def one_row(row, source=source, dest=dest, last=step == SUB):
            mask_x = inside_x(row, REACH, part)
            pieces = [(FRONT, half, None), (FRONT + half, cols - half, None)]
            if not last:
                pieces += [(FRONT - EDGE, EDGE, south_mask), (end, EDGE, north_mask)]
            for start, count, mask_y in pieces:
                value = advance(source, row, start, count, fine_constants)
                mask = mask_x if mask_y is None else jnp.logical_and(mask_x, mask_y)
                if not (last and mask_y is None):
                    value = jnp.where(mask, value, 0.0)
                dest[row, pl.ds(start, count), :] = value

        pl.loop(step, wide - step)(one_row)
        source, dest = dest, source
    fine = source

    for row in range(part_c):
        fine_mean[row] = restricted(fine, row)

    count_c = cols_c + 2 * EDGE
    begin_c = FRONT - EDGE
    mask_y = inside_y(begin_c, count_c, cols_c)

    def extend(buffer):
        for row in range(wide_c):
            here = buffer[row, pl.ds(begin_c, count_c), :]
            if row < COARSE_REACH:
                here = pltpu.roll(
                    jnp.where(high_lanes, here, buffer[row + part_c, pl.ds(begin_c, count_c), :]), levels, 1
                )
            elif row >= COARSE_REACH + part_c:
                here = pltpu.roll(
                    jnp.where(low_lanes, here, buffer[row - part_c, pl.ds(begin_c, count_c), :]), LANES - levels, 1
                )
            mask = jnp.logical_and(mask_y, inside_x(row, COARSE_REACH, part_c))
            extended[row, pl.ds(begin_c, count_c), :] = jnp.where(mask, here, 0.0)

    all_arrived(old_copies, 0, AROUND)
    sends_done(old_copies, 0, AROUND)
    extend(old_wide)
    for row in range(1, wide_c - 1):
        old_image[row - 1] = advance(extended, row, begin_c, count_c, coarse_constants)

    @pl.when(tm > 0)
    def _():
        all_arrived(chain_copies, 1, PLANE)
        extend(new_wide)

    for row in range(1, wide_c - 1):
        moved = advance(extended, row, begin_c, count_c, coarse_constants) - old_image[row - 1]
        mask = jnp.logical_and(mask_y, inside_x(row, COARSE_REACH, part_c))
        change[row - 1, pl.ds(begin_c, count_c), :] = jnp.where(mask, moved, 0.0)

    def change_row(row):
        return change[row, pl.ds(begin_c, count_c), :]

    @pl.when(tm < n_tm - 1)
    def _():
        for row in range(part_c):
            line[pl.ds(begin_c, count_c), :] = (
                mean_side * (change_row(row) + change_row(row + 2)) + mean_mid * change_row(row + 1)
            )
            sides = line[pl.ds(FRONT - 1, cols_c), :] + line[pl.ds(FRONT + 1, cols_c), :]
            sent[row] = fine_mean[row] + mean_side * sides + mean_mid * line[pl.ds(FRONT, cols_c), :]
        send_all(chain_copies, 1, PLANE)

    def blend(offset, low, mid, high):
        total = weights_mid[offset] * mid
        if weights_low[offset]:
            total = total + weights_low[offset] * low
        if weights_high[offset]:
            total = total + weights_high[offset] * high
        return total

    for row in range(part):
        at, offset = row // RATIO, row % RATIO
        line[pl.ds(begin_c, count_c), :] = blend(offset, change_row(at), change_row(at + 1), change_row(at + 2))
        low, mid, high = (line[pl.ds(FRONT + d, cols_c), :] for d in (-1, 0, 1))
        for o in range(RATIO):
            fine_line[pl.ds(o, cols_c, stride=RATIO), :] = blend(o, low, mid, high)
        ending = (fine[REACH + row, pl.ds(FRONT, cols), :] + fine_line[...]).T
        for p in range(packs):
            out_ref[pl.ds(p * part + row, levels, stride=rows), :] = ending[p * levels : (p + 1) * levels]

    pl.when(tm < n_tm - 1)(lambda: sends_done(chain_copies, 1, PLANE))


def shards(sizes, state_starts, diffusivity, wind):
    _, levels, rows, cols = state_starts.shape
    packs = LANES // levels
    part = rows // packs
    part_c = part // RATIO
    cols_c = cols // RATIO
    wide, wide_c = part + 2 * REACH, part_c + 2 * COARSE_REACH
    vmem = functools.partial(pltpu.VMEM, dtype=jnp.float32)
    scratch = [
        vmem((wide, cols + 2 * FRONT, LANES)),
        vmem((wide, cols + 2 * FRONT, LANES)),
        vmem((2, REACH, levels, cols)),
        vmem((2, REACH, levels, cols)),
        vmem((wide_c, cols_c + 2 * FRONT, LANES)),
        vmem((wide_c, cols_c + 2 * FRONT, LANES)),
        vmem((wide_c, cols_c + 2 * FRONT, LANES)),
        vmem((wide_c - 2, cols_c + 2 * EDGE, LANES)),
        vmem((wide_c - 2, cols_c + 2 * FRONT, LANES)),
        vmem((part_c, cols_c, LANES)),
        vmem((part_c, cols_c, LANES)),
        vmem((cols_c + 2 * FRONT, LANES)),
        vmem((cols, LANES)),
    ] + [pltpu.SemaphoreType.DMA((9,))] * 6
    in_vmem = pl.BlockSpec(memory_space=pltpu.VMEM)
    ending = pl.pallas_call(
        functools.partial(kernel, sizes, levels, rows, cols),
        out_shape=jax.ShapeDtypeStruct((levels * rows, cols), jnp.float32),
        in_specs=[in_vmem] * 3,
        out_specs=in_vmem,
        scratch_shapes=scratch,
        compiler_params=pltpu.CompilerParams(collective_id=0, has_side_effects=True),
        name="parareal",
    )(state_starts.reshape(levels * rows, cols), diffusivity.reshape(1, levels), wind)
    return ending.reshape(1, levels, rows, cols)


def solution(mesh):
    sizes = tuple(mesh.shape[axis] for axis in ("tm", "gx", "gy"))
    placed = (P("tm", None, "gx", "gy"), P(), P())
    return jax.shard_map(
        functools.partial(shards, sizes),
        mesh=mesh, in_specs=placed, out_specs=P("tm", None, "gx", "gy"), check_vma=False,
    )
```

time: 200 us -> 31.2 us (0.16)
  the two profiles are of different devices: /device:TPU:25 before, /device:TPU:27 now
where the time goes in v1:
time: 31.2 us; the launch traced here: 31.1 us
  Pallas kernels  28.8 us (92%)
  local copies, waits for them, and re-layouts  2.26 us (7%)
    pallas_call x1, Pallas kernels, shards(): pl.pallas_call(functools.partial(kernel, sizes, levels, rows, cols), out_...  28.8 us
    unnamed x1, local copies, waits for them, and re-layouts  2.26 us

profile of v1, /device:TPU:27, one launch (start us, length us, event | category | flops | bytes accessed | tf_op | source)
XLA Modules:
  0.0 31.1 jit_solution(9403252843522535672)
XLA Ops:
  0.0 28.8 %parareal.1 = f32[2048,128]{1,0:T(8,128)} custom-call(f32[2048,128]{1,0:T(8,128)} %bitcast.4, f32[1,64]{1,0:T(1,128)} %bitcast.5, f32[2,64]{1,0:T(2,128)} %wind_ref.1), custom_call_target="tpu_custom_call" | custom-call | tf_op jit(solution)/shard_map/parareal/pallas_call | solution.py:348
  28.8 2.3 %copy.5 = f32[1,64,32,128]{3,2,1,0:T(8,128)} copy(f32[1,64,32,128]{3,2,1,0:T(8,128)} %bitcast.3) | data formatting | bytes 2097152

commit v2 on v1

--- a/solution.py
+++ b/solution.py
@@ -347,7 +347,7 @@
     in_vmem = pl.BlockSpec(memory_space=pltpu.VMEM)
     ending = pl.pallas_call(
         functools.partial(kernel, sizes, levels, rows, cols),
-        out_shape=jax.ShapeDtypeStruct((levels * rows, cols), jnp.float32),
+        out_shape=pltpu.VMEM((levels * rows, cols), jnp.float32),
         in_specs=[in_vmem] * 3,
         out_specs=in_vmem,
         scratch_shapes=scratch,

time: 31.2 us -> 28.9 us (0.926)
  local copies, waits for them, and re-layouts: 2.26 us -> 0.97 us
  Pallas kernels: 28.8 us -> 27.8 us
    unnamed x1, local copies, waits for them, and re-layouts: 2.26 us -> 0.97 us
    pallas_call x1, Pallas kernels: 28.8 us -> 27.8 us  [shards(): pl.pallas_call(functools.partial(kernel, sizes, levels, rows, cols), out_...]
where the time goes in v2:
time: 28.9 us; the launch traced here: 28.8 us
  Pallas kernels  27.8 us (96%)
  local copies, waits for them, and re-layouts  0.97 us (3%)
    pallas_call x1, Pallas kernels, shards(): pl.pallas_call(functools.partial(kernel, sizes, levels, rows, cols), out_...  27.8 us
    unnamed x1, local copies, waits for them, and re-layouts  0.97 us

profile of v2, /device:TPU:27, one launch (start us, length us, event | category | flops | bytes accessed | tf_op | source)
XLA Modules:
  0.0 28.8 jit_solution(5504839064885298374)
XLA Ops:
  0.0 27.8 %parareal.1 = f32[2048,128]{1,0:T(8,128)S(1)} custom-call(f32[2048,128]{1,0:T(8,128)} %bitcast.4, f32[1,64]{1,0:T(1,128)} %bitcast.5, f32[2,64]{1,0:T(2,128)} %wind_ref.1), custom_call_target="tpu_custom_call" | custom-call | tf_op jit(solution)/shard_map/parareal/pallas_call | solution.py:348
  27.8 1.0 %copy.5 = f32[1,64,32,128]{3,2,1,0:T(8,128)} copy(f32[1,64,32,128]{3,2,1,0:T(8,128)S(1)} %bitcast.3) | data formatting | bytes 2097152

commit v3 on v2

--- a/solution.py
+++ b/solution.py
@@ -34,9 +34,10 @@
 
 def kernel(
     sizes, levels, rows, cols,
-    x_ref, diff_ref, wind_ref, out_ref,
+    x_hbm, diff_ref, wind_ref, out_ref,
+    x_ref, load_sem,
     first, second, x_send, x_recv, old_wide, new_wide, extended, old_image, change,
-    sent, fine_mean, line, fine_line,
+    sent, fine_mean, line, fine_line, raw_edge, spread_rows,
     fine_out, fine_in, old_out, old_in, chain_out, chain_in,
 ):
     n_tm, n_gx, n_gy = sizes
@@ -67,6 +68,9 @@
 
     def target(dz, dx, dy):
         return (tm + dz, gx + dx, gy + dy)
+
+    load = pltpu.make_async_copy(x_hbm, x_ref, load_sem)
+    load.start()
 
     barrier = pltpu.get_barrier_semaphore()
     partners = [(dz, dx, dy) for dz in (-1, 0, 1) for dx, dy in PLANE if (dz, dx, dy) != (0, 0, 0)]
@@ -174,6 +178,7 @@
         stacked = jnp.concatenate([native_row(p * part + row - REACH) for p in range(packs)], axis=0)
         first[row, pl.ds(FRONT, cols), :] = stacked.T
 
+    load.wait()
     for r in range(REACH):
         x_send[0, r] = native_row(r)
         x_send[1, r] = native_row(rows - REACH + r)
@@ -207,48 +212,65 @@
         place = gy * length + (start - FRONT) + lax.broadcasted_iota(jnp.int32, (count, LANES), 0)
         return jnp.logical_and(place >= 0, place < n_gy * length)
 
+    low_lanes = lane < levels
+    high_lanes = lane >= LANES - levels
+    side_moves = tuple(m for m in AROUND if m[0] == 0)
+    corner_moves = tuple(m for m in y_moves if m[0] != 0)
+    edges = ((FRONT - EDGE, inside_y(FRONT - EDGE, EDGE, cols)), (end, inside_y(end, EDGE, cols)))
+    halo_rows = [*range(REACH), *range(REACH + part, wide)]
+    half = cols // 2
+
+    def update(source, dest, row, consts, last):
+        for start, count in ((FRONT, half), (FRONT + half, cols - half)):
+            dest[row, pl.ds(start, count), :] = advance(source, row, start, count, consts)
+        if not last:
+            for start, mask in edges:
+                value = advance(source, row, start, EDGE, consts)
+                dest[row, pl.ds(start, EDGE), :] = jnp.where(mask, value, 0.0)
+
+    buffers = (first, second)
+
+    all_arrived(fine_copies, 0, side_moves)
+    def edge_of(start):
+        return 0 if start < FRONT else 1
+
+    for start, mask in edges:
+        for row in [*range(REACH), *range(part - REACH, part)]:
+            raw_edge[edge_of(start), row] = first[row + REACH, pl.ds(start, EDGE), :]
+        for row in range(REACH, REACH + part):
+            first[row, pl.ds(start, EDGE), :] = jnp.where(mask, first[row, pl.ds(start, EDGE), :], 0.0)
+    for step in range(1, SUB + 1):
+        def inner_row(row, step=step):
+            update(buffers[(step - 1) % 2], buffers[step % 2], row, fine_constants, step == SUB)
+
+        sends_done(fine_copies, 0, y_moves) if step == 2 else None
+        pl.loop(REACH + step, REACH + part - step)(inner_row)
+
     all_arrived(fine_copies, 0, x_moves)
-    for row in [*range(REACH), *range(REACH + part, wide)]:
+    for row in halo_rows:
         bring_in(row)
         inner = first[row, pl.ds(FRONT, cols), :]
         first[row, pl.ds(FRONT, cols), :] = jnp.where(inside_x(row, REACH, part), inner, 0.0)
-    all_arrived(fine_copies, 0, y_moves)
-    sends_done(fine_copies, 0, AROUND)
-    low_lanes = lane < levels
-    high_lanes = lane >= LANES - levels
-    for start in (FRONT - EDGE, end):
-        mask_y = inside_y(start, EDGE, cols)
-        for row in [*range(REACH), *range(REACH + part, wide), *range(REACH, REACH + part)]:
+    all_arrived(fine_copies, 0, corner_moves)
+    for start, mask_y in edges:
+        for row in halo_rows:
             here = first[row, pl.ds(start, EDGE), :]
             if row < REACH:
-                here = pltpu.roll(jnp.where(high_lanes, here, first[row + part, pl.ds(start, EDGE), :]), levels, 1)
-            elif row >= REACH + part:
-                here = pltpu.roll(jnp.where(low_lanes, here, first[row - part, pl.ds(start, EDGE), :]), LANES - levels, 1)
-            mask = mask_y
-            if not REACH <= row < REACH + part:
-                mask = jnp.logical_and(mask, inside_x(row, REACH, part))
+                here = pltpu.roll(jnp.where(high_lanes, here, raw_edge[edge_of(start), row + part - REACH]), levels, 1)
+            else:
+                here = pltpu.roll(jnp.where(low_lanes, here, raw_edge[edge_of(start), row - part - REACH]), LANES - levels, 1)
+            mask = jnp.logical_and(mask_y, inside_x(row, REACH, part))
             first[row, pl.ds(start, EDGE), :] = jnp.where(mask, here, 0.0)
-
-    south_mask = inside_y(FRONT - EDGE, EDGE, cols)
-    north_mask = inside_y(end, EDGE, cols)
-    half = cols // 2
-    source, dest = first, second
     for step in range(1, SUB + 1):
-        def one_row(row, source=source, dest=dest, last=step == SUB):
-            mask_x = inside_x(row, REACH, part)
-            pieces = [(FRONT, half, None), (FRONT + half, cols - half, None)]
-            if not last:
-                pieces += [(FRONT - EDGE, EDGE, south_mask), (end, EDGE, north_mask)]
-            for start, count, mask_y in pieces:
-                value = advance(source, row, start, count, fine_constants)
-                mask = mask_x if mask_y is None else jnp.logical_and(mask_x, mask_y)
-                if not (last and mask_y is None):
-                    value = jnp.where(mask, value, 0.0)
-                dest[row, pl.ds(start, count), :] = value
-
-        pl.loop(step, wide - step)(one_row)
-        source, dest = dest, source
-    fine = source
+        def outer_row(row, step=step):
+            for shifted in (row, row + part + REACH - 2 * step):
+                mask_x = inside_x(shifted, REACH, part)
+                consts = tuple(jnp.where(mask_x, c, 0.0) for c in fine_constants)
+                update(buffers[(step - 1) % 2], buffers[step % 2], shifted, consts, step == SUB)
+
+        pl.loop(step, REACH + step)(outer_row)
+    sends_done(fine_copies, 0, x_moves)
+    fine = buffers[SUB % 2]
 
     for row in range(part_c):
         fine_mean[row] = restricted(fine, row)
@@ -277,8 +299,15 @@
     for row in range(1, wide_c - 1):
         old_image[row - 1] = advance(extended, row, begin_c, count_c, coarse_constants)
 
+    def write_fine():
+        for row in range(part):
+            turned = fine[REACH + row, pl.ds(FRONT, cols), :].T
+            for p in range(packs):
+                out_ref[pl.ds(p * part + row, levels, stride=rows), :] = turned[p * levels : (p + 1) * levels]
+
     @pl.when(tm > 0)
     def _():
+        write_fine()
         all_arrived(chain_copies, 1, PLANE)
         extend(new_wide)
 
@@ -300,23 +329,32 @@
             sent[row] = fine_mean[row] + mean_side * sides + mean_mid * line[pl.ds(FRONT, cols_c), :]
         send_all(chain_copies, 1, PLANE)
 
-    def blend(offset, low, mid, high):
-        total = weights_mid[offset] * mid
-        if weights_low[offset]:
-            total = total + weights_low[offset] * low
-        if weights_high[offset]:
-            total = total + weights_high[offset] * high
-        return total
+    pl.when(tm == 0)(write_fine)
+
+    coarse_col = lax.broadcasted_iota(jnp.int32, (count_c, cols), 0) - EDGE
+    fine_col = lax.broadcasted_iota(jnp.int32, (count_c, cols), 1)
+    offset_of = fine_col & (RATIO - 1)
+    apart = coarse_col - (fine_col >> (RATIO.bit_length() - 1))
+    spreading = jnp.zeros((count_c, cols), jnp.float32)
+    for o in range(RATIO):
+        for distance, weights in ((-1, weights_low), (0, weights_mid), (1, weights_high)):
+            chosen = jnp.logical_and(offset_of == o, apart == distance)
+            spreading = jnp.where(chosen, weights[o], spreading)
+    for row in range(part_c + 2):
+        spread_rows[row] = jnp.dot(
+            change_row(row).T, spreading, precision=lax.Precision.HIGHEST, preferred_element_type=jnp.float32
+        )
 
     for row in range(part):
-        at, offset = row // RATIO, row % RATIO
-        line[pl.ds(begin_c, count_c), :] = blend(offset, change_row(at), change_row(at + 1), change_row(at + 2))
-        low, mid, high = (line[pl.ds(FRONT + d, cols_c), :] for d in (-1, 0, 1))
-        for o in range(RATIO):
-            fine_line[pl.ds(o, cols_c, stride=RATIO), :] = blend(o, low, mid, high)
-        ending = (fine[REACH + row, pl.ds(FRONT, cols), :] + fine_line[...]).T
+        at, o = row // RATIO, row % RATIO
+        total = weights_mid[o] * spread_rows[at + 1]
+        if weights_low[o]:
+            total = total + weights_low[o] * spread_rows[at]
+        if weights_high[o]:
+            total = total + weights_high[o] * spread_rows[at + 2]
         for p in range(packs):
-            out_ref[pl.ds(p * part + row, levels, stride=rows), :] = ending[p * levels : (p + 1) * levels]
+            place = pl.ds(p * part + row, levels, stride=rows)
+            out_ref[place, :] = out_ref[place, :] + total[p * levels : (p + 1) * levels]
 
     pl.when(tm < n_tm - 1)(lambda: sends_done(chain_copies, 1, PLANE))
 
@@ -330,6 +368,8 @@
     wide, wide_c = part + 2 * REACH, part_c + 2 * COARSE_REACH
     vmem = functools.partial(pltpu.VMEM, dtype=jnp.float32)
     scratch = [
+        vmem((levels * rows, cols)),
+        pltpu.SemaphoreType.DMA,
         vmem((wide, cols + 2 * FRONT, LANES)),
         vmem((wide, cols + 2 * FRONT, LANES)),
         vmem((2, REACH, levels, cols)),
@@ -343,12 +383,14 @@
         vmem((part_c, cols_c, LANES)),
         vmem((cols_c + 2 * FRONT, LANES)),
         vmem((cols, LANES)),
+        vmem((2, part, EDGE, LANES)),
+        vmem((part_c + 2, LANES, cols)),
     ] + [pltpu.SemaphoreType.DMA((9,))] * 6
     in_vmem = pl.BlockSpec(memory_space=pltpu.VMEM)
     ending = pl.pallas_call(
         functools.partial(kernel, sizes, levels, rows, cols),
         out_shape=pltpu.VMEM((levels * rows, cols), jnp.float32),
-        in_specs=[in_vmem] * 3,
+        in_specs=[pl.BlockSpec(memory_space=pl.ANY), in_vmem, in_vmem],
         out_specs=in_vmem,
         scratch_shapes=scratch,
         compiler_params=pltpu.CompilerParams(collective_id=0, has_side_effects=True),

time: 28.9 us -> 27.2 us (0.941)
  Pallas kernels: 27.8 us -> 26.1 us
    pallas_call x1, Pallas kernels: 27.8 us -> 26.1 us  [shards(): pl.pallas_call(functools.partial(kernel, sizes, levels, rows, cols), out_...]
where the time goes in v3:
time: 27.2 us; the launch traced here: 27.1 us
  Pallas kernels  26.1 us (96%)
  local copies, waits for them, and re-layouts  0.97 us (4%)
    pallas_call x1, Pallas kernels, shards(): pl.pallas_call(functools.partial(kernel, sizes, levels, rows, cols), out_...  26.1 us
    unnamed x1, local copies, waits for them, and re-layouts  0.97 us

profile of v3, /device:TPU:27, one launch (start us, length us, event | category | flops | bytes accessed | tf_op | source)
XLA Modules:
  0.0 27.1 jit_solution(16854038026735327298)
XLA Ops:
  0.0 26.1 %parareal.1 = f32[2048,128]{1,0:T(8,128)S(1)} custom-call(f32[2048,128]{1,0:T(8,128)} %bitcast.4, f32[1,64]{1,0:T(1,128)} %bitcast.5, f32[2,64]{1,0:T(2,128)} %wind_ref.1), custom_call_target="tpu_custom_call" | custom-call | tf_op jit(solution)/shard_map/parareal/pallas_call | solution.py:390
  26.1 1.0 %copy.5 = f32[1,64,32,128]{3,2,1,0:T(8,128)} copy(f32[1,64,32,128]{3,2,1,0:T(8,128)S(1)} %bitcast.3) | data formatting | bytes 2097152

commit v4 on v3

--- a/solution.py
+++ b/solution.py
@@ -38,7 +38,7 @@
     x_ref, load_sem,
     first, second, x_send, x_recv, old_wide, new_wide, extended, old_image, change,
     sent, fine_mean, line, fine_line, raw_edge, spread_rows,
-    fine_out, fine_in, old_out, old_in, chain_out, chain_in,
+    fine_out, fine_in, old_out, old_in, chain_out, chain_in, *strip_refs,
 ):
     n_tm, n_gx, n_gy = sizes
     tm, gx, gy = lax.axis_index("tm"), lax.axis_index("gx"), lax.axis_index("gy")
@@ -74,6 +74,7 @@
 
     barrier = pltpu.get_barrier_semaphore()
     partners = [(dz, dx, dy) for dz in (-1, 0, 1) for dx, dy in PLANE if (dz, dx, dy) != (0, 0, 0)]
+    partners.sort(key=lambda move: -sum(map(abs, move)))
     awaited = jnp.int32(0)
     for move in partners:
         def greet(move=move):
@@ -117,28 +118,26 @@
             landing = first.at[pl.ds(put_row, height), pl.ds(put, EDGE)]
         fine_copies[move] = remote(source, landing, fine_out.at[k], fine_in.at[k], (0, dx, dy))
 
-    def coarse_copies(buffer, row0, col0, landing_buffer, out_sems, in_sems, dz, moves):
+    def coarse_copies(main, wide_in, strips, out_sems, in_sems, dz):
+        row_out, row_in, side_out, side_in, corner_out, corner_in = strips
         copies = {}
-        for move in moves:
-            dx, dy = move
-            k = index_of(move)
-            take_row, put_row, height = {
-                0: (0, COARSE_REACH, part_c),
-                -1: (0, COARSE_REACH + part_c, COARSE_REACH),
-                1: (part_c - COARSE_REACH, 0, COARSE_REACH),
-            }[dx]
-            take, put, width = {
-                0: (0, FRONT, cols_c), -1: (0, end_c, EDGE), 1: (cols_c - EDGE, FRONT - EDGE, EDGE)
-            }[dy]
-            copies[move] = remote(
-                buffer.at[pl.ds(row0 + take_row, height), pl.ds(col0 + take, width)],
-                landing_buffer.at[pl.ds(put_row, height), pl.ds(put, width)],
-                out_sems.at[k], in_sems.at[k], (dz, dx, dy),
-            )
+        for dx, dy in PLANE if dz else AROUND:
+            k = index_of((dx, dy))
+            towards_x, towards_y = (dx + 1) // 2, (dy + 1) // 2
+            if dx == 0 and dy == 0:
+                source, landing = main, wide_in.at[pl.ds(COARSE_REACH, part_c), pl.ds(FRONT, cols_c)]
+            elif dy == 0:
+                source, landing = row_out.at[towards_x], row_in.at[towards_x, pl.ds(FRONT, cols_c)]
+            elif dx == 0:
+                source, landing = side_out.at[towards_y], side_in.at[towards_y]
+            else:
+                source, landing = corner_out.at[towards_x, towards_y], corner_in.at[towards_x, towards_y]
+            copies[dx, dy] = remote(source, landing, out_sems.at[k], in_sems.at[k], (dz, dx, dy))
         return copies
 
-    old_copies = coarse_copies(old_wide, COARSE_REACH, FRONT, old_wide, old_out, old_in, 0, AROUND)
-    chain_copies = coarse_copies(sent, 0, 0, new_wide, chain_out, chain_in, 1, PLANE)
+    old_strips, new_strips = strip_refs[:6], strip_refs[6:]
+    old_copies = coarse_copies(None, old_wide, old_strips, old_out, old_in, 0)
+    chain_copies = coarse_copies(sent, new_wide, new_strips, chain_out, chain_in, 1)
 
     lane = lax.broadcasted_iota(jnp.int32, (1, LANES), 1)
     pack = lane // levels
@@ -182,13 +181,12 @@
     for r in range(REACH):
         x_send[0, r] = native_row(r)
         x_send[1, r] = native_row(rows - REACH + r)
-    pl.semaphore_wait(barrier, awaited)
     x_moves = tuple(m for m in AROUND if m[1] == 0)
     y_moves = tuple(m for m in AROUND if m[1] != 0)
-    send_all(fine_copies, 0, x_moves)
+    low_lanes = lane < levels
+    high_lanes = lane >= LANES - levels
     for row in range(REACH, REACH + part):
         bring_in(row)
-    send_all(fine_copies, 0, y_moves)
 
     def restricted(source, row):
         total = source[REACH + row * RATIO, pl.ds(FRONT, cols), :]
@@ -200,8 +198,28 @@
             mean = mean + fine_line[pl.ds(o, cols_c, stride=RATIO), :]
         return mean * (1.0 / RATIO**2)
 
+    def swapped(value):
+        return pltpu.roll(value, levels, 1)
+
+    def pack_strips(row_of, strips):
+        row_out, _, side_out, _, corner_out, _ = strips
+        row_out[0] = jnp.where(low_lanes, row_of(0, 0, cols_c), swapped(row_of(1, 0, cols_c)))
+        row_out[1] = jnp.where(low_lanes, swapped(row_of(part_c - 2, 0, cols_c)), row_of(part_c - 1, 0, cols_c))
+        for side, col in ((0, 0), (1, cols_c - COARSE_REACH)):
+            for row in range(part_c):
+                side_out[side, pl.ds(COARSE_REACH * row, COARSE_REACH), :] = row_of(row, col, COARSE_REACH)
+            for towards in range(2):
+                corner_out[towards, side, pl.ds(0, COARSE_REACH), :] = row_out[towards, pl.ds(col, COARSE_REACH), :]
+
+    def old_row(row, col, count):
+        return old_wide[COARSE_REACH + row, pl.ds(FRONT + col, count), :]
+
     for row in range(part_c):
         old_wide[COARSE_REACH + row, pl.ds(FRONT, cols_c), :] = restricted(first, row)
+    pack_strips(old_row, old_strips)
+    pl.semaphore_wait(barrier, awaited)
+    send_all(fine_copies, 0, y_moves)
+    send_all(fine_copies, 0, x_moves)
     send_all(old_copies, 0, AROUND)
 
     def inside_x(row, reach, length):
@@ -212,8 +230,6 @@
         place = gy * length + (start - FRONT) + lax.broadcasted_iota(jnp.int32, (count, LANES), 0)
         return jnp.logical_and(place >= 0, place < n_gy * length)
 
-    low_lanes = lane < levels
-    high_lanes = lane >= LANES - levels
     side_moves = tuple(m for m in AROUND if m[0] == 0)
     corner_moves = tuple(m for m in y_moves if m[0] != 0)
     edges = ((FRONT - EDGE, inside_y(FRONT - EDGE, EDGE, cols)), (end, inside_y(end, EDGE, cols)))
@@ -279,23 +295,36 @@
     begin_c = FRONT - EDGE
     mask_y = inside_y(begin_c, count_c, cols_c)
 
-    def extend(buffer):
-        for row in range(wide_c):
-            here = buffer[row, pl.ds(begin_c, count_c), :]
-            if row < COARSE_REACH:
-                here = pltpu.roll(
-                    jnp.where(high_lanes, here, buffer[row + part_c, pl.ds(begin_c, count_c), :]), levels, 1
-                )
-            elif row >= COARSE_REACH + part_c:
-                here = pltpu.roll(
-                    jnp.where(low_lanes, here, buffer[row - part_c, pl.ds(begin_c, count_c), :]), LANES - levels, 1
-                )
-            mask = jnp.logical_and(mask_y, inside_x(row, COARSE_REACH, part_c))
-            extended[row, pl.ds(begin_c, count_c), :] = jnp.where(mask, here, 0.0)
+    def extend(buffer, strips):
+        _, row_in, _, side_in, _, corner_in = strips
+        for side, col in ((0, end_c), (1, FRONT - COARSE_REACH)):
+            for row in range(part_c):
+                buffer[COARSE_REACH + row, pl.ds(col, COARSE_REACH), :] = side_in[
+                    side, pl.ds(COARSE_REACH * row, COARSE_REACH), :
+                ]
+            for towards in range(2):
+                row_in[towards, pl.ds(col, COARSE_REACH), :] = corner_in[towards, side, pl.ds(0, COARSE_REACH), :]
+
+        def own(row):
+            return buffer[COARSE_REACH + row, pl.ds(begin_c, count_c), :]
+
+        above, below = (row_in[towards, pl.ds(begin_c, count_c), :] for towards in (0, 1))
+        values = [
+            jnp.where(low_lanes, below, swapped(own(part_c - 2))),
+            swapped(jnp.where(high_lanes, below, own(part_c - 1))),
+            *[own(row) for row in range(part_c)],
+            swapped(jnp.where(low_lanes, above, own(0))),
+            jnp.where(high_lanes, above, swapped(own(1))),
+        ]
+        for row, value in enumerate(values):
+            mask = mask_y
+            if not COARSE_REACH <= row < COARSE_REACH + part_c:
+                mask = jnp.logical_and(mask_y, inside_x(row, COARSE_REACH, part_c))
+            extended[row, pl.ds(begin_c, count_c), :] = jnp.where(mask, value, 0.0)
 
     all_arrived(old_copies, 0, AROUND)
     sends_done(old_copies, 0, AROUND)
-    extend(old_wide)
+    extend(old_wide, old_strips)
     for row in range(1, wide_c - 1):
         old_image[row - 1] = advance(extended, row, begin_c, count_c, coarse_constants)
 
@@ -309,7 +338,7 @@
     def _():
         write_fine()
         all_arrived(chain_copies, 1, PLANE)
-        extend(new_wide)
+        extend(new_wide, new_strips)
 
     for row in range(1, wide_c - 1):
         moved = advance(extended, row, begin_c, count_c, coarse_constants) - old_image[row - 1]
@@ -327,7 +356,9 @@
             )
             sides = line[pl.ds(FRONT - 1, cols_c), :] + line[pl.ds(FRONT + 1, cols_c), :]
             sent[row] = fine_mean[row] + mean_side * sides + mean_mid * line[pl.ds(FRONT, cols_c), :]
-        send_all(chain_copies, 1, PLANE)
+        pack_strips(lambda row, col, count: sent[row, pl.ds(col, count), :], new_strips)
+        send_all(chain_copies, 1, AROUND)
+        send_all(chain_copies, 1, ((0, 0),))
 
     pl.when(tm == 0)(write_fine)
 
@@ -362,6 +393,8 @@
 def shards(sizes, state_starts, diffusivity, wind):
     _, levels, rows, cols = state_starts.shape
     packs = LANES // levels
+    if packs != 2 or levels * packs != LANES:
+        raise ValueError(levels)
     part = rows // packs
     part_c = part // RATIO
     cols_c = cols // RATIO
@@ -386,6 +419,14 @@
         vmem((2, part, EDGE, LANES)),
         vmem((part_c + 2, LANES, cols)),
     ] + [pltpu.SemaphoreType.DMA((9,))] * 6
+    scratch += [
+        vmem((2, cols_c, LANES)),
+        vmem((2, cols_c + 2 * FRONT, LANES)),
+        vmem((2, COARSE_REACH * part_c, LANES)),
+        vmem((2, COARSE_REACH * part_c, LANES)),
+        vmem((2, 2, EDGE, LANES)),
+        vmem((2, 2, EDGE, LANES)),
+    ] * 2
     in_vmem = pl.BlockSpec(memory_space=pltpu.VMEM)
     ending = pl.pallas_call(
         functools.partial(kernel, sizes, levels, rows, cols),

time: 27.2 us -> 24.6 us (0.904)
  the two profiles are of different devices: /device:TPU:27 before, /device:TPU:25 now
where the time goes in v4:
time: 24.6 us; the launch traced here: 24.4 us
  Pallas kernels  23.4 us (95%)
  local copies, waits for them, and re-layouts  0.97 us (4%)
    pallas_call x1, Pallas kernels, shards(): pl.pallas_call(functools.partial(kernel, sizes, levels, rows, cols), out_...  23.4 us
    unnamed x1, local copies, waits for them, and re-layouts  0.97 us

profile of v4, /device:TPU:25, one launch (start us, length us, event | category | flops | bytes accessed | tf_op | source)
XLA Modules:
  0.0 24.4 jit_solution(16095301713299574202)
XLA Ops:
  0.0 23.4 %parareal.1 = f32[2048,128]{1,0:T(8,128)S(1)} custom-call(f32[2048,128]{1,0:T(8,128)} %bitcast.4, f32[1,64]{1,0:T(1,128)} %bitcast.5, f32[2,64]{1,0:T(2,128)} %wind_ref.1), custom_call_target="tpu_custom_call" | custom-call | tf_op jit(solution)/shard_map/parareal/pallas_call | solution.py:431
  23.4 1.0 %copy.5 = f32[1,64,32,128]{3,2,1,0:T(8,128)} copy(f32[1,64,32,128]{3,2,1,0:T(8,128)S(1)} %bitcast.3) | data formatting | bytes 2097152

commit v5 on v4

--- a/solution.py
+++ b/solution.py
@@ -37,7 +37,7 @@
     x_hbm, diff_ref, wind_ref, out_ref,
     x_ref, load_sem,
     first, second, x_send, x_recv, old_wide, new_wide, extended, old_image, change,
-    sent, fine_mean, line, fine_line, raw_edge, spread_rows,
+    sent, fine_mean, line, fine_line, raw_edge, spread_rows, turned,
     fine_out, fine_in, old_out, old_in, chain_out, chain_in, *strip_refs,
 ):
     n_tm, n_gx, n_gy = sizes
@@ -260,7 +260,7 @@
             update(buffers[(step - 1) % 2], buffers[step % 2], row, fine_constants, step == SUB)
 
         sends_done(fine_copies, 0, y_moves) if step == 2 else None
-        pl.loop(REACH + step, REACH + part - step)(inner_row)
+        pl.loop(REACH + step, REACH + part - step, unroll=2)(inner_row)
 
     all_arrived(fine_copies, 0, x_moves)
     for row in halo_rows:
@@ -330,9 +330,7 @@
 
     def write_fine():
         for row in range(part):
-            turned = fine[REACH + row, pl.ds(FRONT, cols), :].T
-            for p in range(packs):
-                out_ref[pl.ds(p * part + row, levels, stride=rows), :] = turned[p * levels : (p + 1) * levels]
+            turned[row] = fine[REACH + row, pl.ds(FRONT, cols), :].T
 
     @pl.when(tm > 0)
     def _():
@@ -371,21 +369,25 @@
         for distance, weights in ((-1, weights_low), (0, weights_mid), (1, weights_high)):
             chosen = jnp.logical_and(offset_of == o, apart == distance)
             spreading = jnp.where(chosen, weights[o], spreading)
+    spreading = jnp.concatenate([spreading.astype(jnp.bfloat16)] * 3, axis=0)
     for row in range(part_c + 2):
-        spread_rows[row] = jnp.dot(
-            change_row(row).T, spreading, precision=lax.Precision.HIGHEST, preferred_element_type=jnp.float32
-        )
+        rest, pieces = change_row(row), []
+        for _ in range(3):
+            piece = rest.astype(jnp.bfloat16).astype(jnp.float32)
+            pieces.append(piece)
+            rest = rest - piece
+        split = jnp.concatenate(pieces, axis=0).T.astype(jnp.bfloat16)
+        spread_rows[row] = jnp.dot(split, spreading, preferred_element_type=jnp.float32)
 
     for row in range(part):
         at, o = row // RATIO, row % RATIO
-        total = weights_mid[o] * spread_rows[at + 1]
+        total = turned[row] + weights_mid[o] * spread_rows[at + 1]
         if weights_low[o]:
             total = total + weights_low[o] * spread_rows[at]
         if weights_high[o]:
             total = total + weights_high[o] * spread_rows[at + 2]
         for p in range(packs):
-            place = pl.ds(p * part + row, levels, stride=rows)
-            out_ref[place, :] = out_ref[place, :] + total[p * levels : (p + 1) * levels]
+            out_ref[pl.ds(p * part + row, levels, stride=rows), :] = total[p * levels : (p + 1) * levels]
 
     pl.when(tm < n_tm - 1)(lambda: sends_done(chain_copies, 1, PLANE))
 
@@ -418,6 +420,7 @@
         vmem((cols, LANES)),
         vmem((2, part, EDGE, LANES)),
         vmem((part_c + 2, LANES, cols)),
+        vmem((part, LANES, cols)),
     ] + [pltpu.SemaphoreType.DMA((9,))] * 6
     scratch += [
         vmem((2, cols_c, LANES)),

time: 24.6 us -> 23.9 us (0.972)
  Pallas kernels: 23.4 us -> 22.8 us
    pallas_call x1, Pallas kernels: 23.4 us -> 22.8 us  [shards(): pl.pallas_call(functools.partial(kernel, sizes, levels, rows, cols), out_...]
where the time goes in v5:
time: 23.9 us; the launch traced here: 23.8 us
  Pallas kernels  22.8 us (95%)
  local copies, waits for them, and re-layouts  0.97 us (4%)
    pallas_call x1, Pallas kernels, shards(): pl.pallas_call(functools.partial(kernel, sizes, levels, rows, cols), out_...  22.8 us
    unnamed x1, local copies, waits for them, and re-layouts  0.97 us

profile of v5, /device:TPU:25, one launch (start us, length us, event | category | flops | bytes accessed | tf_op | source)
XLA Modules:
  0.0 23.8 jit_solution(8401225736906661390)
XLA Ops:
  0.0 22.8 %parareal.1 = f32[2048,128]{1,0:T(8,128)S(1)} custom-call(f32[2048,128]{1,0:T(8,128)} %bitcast.4, f32[1,64]{1,0:T(1,128)} %bitcast.5, f32[2,64]{1,0:T(2,128)} %wind_ref.1), custom_call_target="tpu_custom_call" | custom-call | tf_op jit(solution)/shard_map/parareal/pallas_call | solution.py:434
  22.8 1.0 %copy.5 = f32[1,64,32,128]{3,2,1,0:T(8,128)} copy(f32[1,64,32,128]{3,2,1,0:T(8,128)S(1)} %bitcast.3) | data formatting | bytes 2097152

commit v6 on v5

--- a/solution.py
+++ b/solution.py
@@ -36,7 +36,7 @@
     sizes, levels, rows, cols,
     x_hbm, diff_ref, wind_ref, out_ref,
     x_ref, load_sem,
-    first, second, x_send, x_recv, old_wide, new_wide, extended, old_image, change,
+    first, second, x_recv, old_wide, new_wide, extended, old_image, change,
     sent, fine_mean, line, fine_line, raw_edge, spread_rows, turned,
     fine_out, fine_in, old_out, old_in, chain_out, chain_in, *strip_refs,
 ):
@@ -69,8 +69,9 @@
     def target(dz, dx, dy):
         return (tm + dz, gx + dx, gy + dy)
 
-    load = pltpu.make_async_copy(x_hbm, x_ref, load_sem)
-    load.start()
+    loads = [pltpu.make_async_copy(x_hbm.at[:, x], x_ref.at[x], load_sem.at[x]) for x in range(rows)]
+    for x in sorted(range(rows), key=lambda x: min(x, rows - 1 - x) >= REACH):
+        loads[x].start()
 
     barrier = pltpu.get_barrier_semaphore()
     partners = [(dz, dx, dy) for dz in (-1, 0, 1) for dx, dy in PLANE if (dz, dx, dy) != (0, 0, 0)]
@@ -108,7 +109,7 @@
         dx, dy = move
         k = index_of(move)
         if dy == 0:
-            source, landing = x_send.at[(dx + 1) // 2], x_recv.at[(dx + 1) // 2]
+            source, landing = x_ref.at[pl.ds((0, 0, rows - REACH)[dx + 1], REACH)], x_recv.at[(dx + 1) // 2]
         else:
             take_row, put_row, height = {
                 0: (REACH, REACH, part), -1: (REACH, REACH + part, REACH), 1: (part, 0, REACH)
@@ -171,16 +172,14 @@
             return x_recv[1, x + REACH]
         if x >= rows:
             return x_recv[0, x - rows]
-        return x_ref[pl.ds(x, levels, stride=rows), :]
+        return x_ref[x]
 
     def bring_in(row):
         stacked = jnp.concatenate([native_row(p * part + row - REACH) for p in range(packs)], axis=0)
         first[row, pl.ds(FRONT, cols), :] = stacked.T
 
-    load.wait()
-    for r in range(REACH):
-        x_send[0, r] = native_row(r)
-        x_send[1, r] = native_row(rows - REACH + r)
+    for load in loads:
+        load.wait()
     x_moves = tuple(m for m in AROUND if m[1] == 0)
     y_moves = tuple(m for m in AROUND if m[1] != 0)
     low_lanes = lane < levels
@@ -218,8 +217,8 @@
         old_wide[COARSE_REACH + row, pl.ds(FRONT, cols_c), :] = restricted(first, row)
     pack_strips(old_row, old_strips)
     pl.semaphore_wait(barrier, awaited)
+    send_all(fine_copies, 0, x_moves)
     send_all(fine_copies, 0, y_moves)
-    send_all(fine_copies, 0, x_moves)
     send_all(old_copies, 0, AROUND)
 
     def inside_x(row, reach, length):
@@ -403,11 +402,10 @@
     wide, wide_c = part + 2 * REACH, part_c + 2 * COARSE_REACH
     vmem = functools.partial(pltpu.VMEM, dtype=jnp.float32)
     scratch = [
-        vmem((levels * rows, cols)),
-        pltpu.SemaphoreType.DMA,
+        vmem((rows, levels, cols)),
+        pltpu.SemaphoreType.DMA((rows,)),
         vmem((wide, cols + 2 * FRONT, LANES)),
         vmem((wide, cols + 2 * FRONT, LANES)),
-        vmem((2, REACH, levels, cols)),
         vmem((2, REACH, levels, cols)),
         vmem((wide_c, cols_c + 2 * FRONT, LANES)),
         vmem((wide_c, cols_c + 2 * FRONT, LANES)),
@@ -439,7 +437,7 @@
         scratch_shapes=scratch,
         compiler_params=pltpu.CompilerParams(collective_id=0, has_side_effects=True),
         name="parareal",
-    )(state_starts.reshape(levels * rows, cols), diffusivity.reshape(1, levels), wind)
+    )(state_starts[0], diffusivity.reshape(1, levels), wind)
     return ending.reshape(1, levels, rows, cols)
 
 

time: 23.9 us -> 24.2 us (1.013)
  no operation moved by 1% of the time
where the time goes in v6:
time: 24.2 us; the launch traced here: 23.9 us
  Pallas kernels  22.9 us (95%)
  local copies, waits for them, and re-layouts  0.97 us (4%)
    pallas_call x1, Pallas kernels, shards(): pl.pallas_call(functools.partial(kernel, sizes, levels, rows, cols), out_...  22.9 us
    unnamed x1, local copies, waits for them, and re-layouts  0.97 us

profile of v6, /device:TPU:25, one launch (start us, length us, event | category | flops | bytes accessed | tf_op | source)
XLA Modules:
  0.0 23.9 jit_solution(349538925553092142)
XLA Ops:
  0.0 22.9 %parareal.1 = f32[2048,128]{1,0:T(8,128)S(1)} custom-call(f32[64,32,128]{2,1,0:T(8,128)} %bitcast.4, f32[1,64]{1,0:T(1,128)} %bitcast.5, f32[2,64]{1,0:T(2,128)} %wind_ref.1), custom_call_target="tpu_custom_call" | custom-call | tf_op jit(solution)/shard_map/parareal/pallas_call | solution.py:432
  22.9 1.0 %copy.5 = f32[1,64,32,128]{3,2,1,0:T(8,128)} copy(f32[1,64,32,128]{3,2,1,0:T(8,128)S(1)} %bitcast.3) | data formatting | bytes 2097152

commit v7 on v5

--- a/solution.py
+++ b/solution.py
@@ -35,7 +35,7 @@
 def kernel(
     sizes, levels, rows, cols,
     x_hbm, diff_ref, wind_ref, out_ref,
-    x_ref, load_sem,
+    x_ref, load_sem, ready,
     first, second, x_send, x_recv, old_wide, new_wide, extended, old_image, change,
     sent, fine_mean, line, fine_line, raw_edge, spread_rows, turned,
     fine_out, fine_in, old_out, old_in, chain_out, chain_in, *strip_refs,
@@ -73,7 +73,7 @@
     load.start()
 
     barrier = pltpu.get_barrier_semaphore()
-    partners = [(dz, dx, dy) for dz in (-1, 0, 1) for dx, dy in PLANE if (dz, dx, dy) != (0, 0, 0)]
+    partners = [(0, dx, dy) for dx, dy in AROUND] + [(-1, 0, 0), (1, 0, 0)]
     partners.sort(key=lambda move: -sum(map(abs, move)))
     awaited = jnp.int32(0)
     for move in partners:
@@ -218,6 +218,11 @@
         old_wide[COARSE_REACH + row, pl.ds(FRONT, cols_c), :] = restricted(first, row)
     pack_strips(old_row, old_strips)
     pl.semaphore_wait(barrier, awaited)
+
+    @pl.when(tm > 0)
+    def _():
+        pl.semaphore_signal(ready, inc=1, device_id=target(-1, 0, 0), device_id_type=pl.DeviceIdType.MESH)
+
     send_all(fine_copies, 0, y_moves)
     send_all(fine_copies, 0, x_moves)
     send_all(old_copies, 0, AROUND)
@@ -328,6 +333,8 @@
     for row in range(1, wide_c - 1):
         old_image[row - 1] = advance(extended, row, begin_c, count_c, coarse_constants)
 
+    pl.when(tm < n_tm - 1)(lambda: pl.semaphore_wait(ready, 1))
+
     def write_fine():
         for row in range(part):
             turned[row] = fine[REACH + row, pl.ds(FRONT, cols), :].T
@@ -405,6 +412,7 @@
     scratch = [
         vmem((levels * rows, cols)),
         pltpu.SemaphoreType.DMA,
+        pltpu.SemaphoreType.REGULAR,
         vmem((wide, cols + 2 * FRONT, LANES)),
         vmem((wide, cols + 2 * FRONT, LANES)),
         vmem((2, REACH, levels, cols)),

time: 23.9 us -> 23.3 us (0.975)
  Pallas kernels: 22.8 us -> 22.2 us
    pallas_call x1, Pallas kernels: 22.8 us -> 22.2 us  [shards(): pl.pallas_call(functools.partial(kernel, sizes, levels, rows, cols), out_...]
where the time goes in v7:
time: 23.3 us; the launch traced here: 23.2 us
  Pallas kernels  22.2 us (95%)
  local copies, waits for them, and re-layouts  0.97 us (4%)
    pallas_call x1, Pallas kernels, shards(): pl.pallas_call(functools.partial(kernel, sizes, levels, rows, cols), out_...  22.2 us
    unnamed x1, local copies, waits for them, and re-layouts  0.97 us

profile of v7, /device:TPU:25, one launch (start us, length us, event | category | flops | bytes accessed | tf_op | source)
XLA Modules:
  0.0 23.2 jit_solution(4083718173078008263)
XLA Ops:
  0.0 22.2 %parareal.1 = f32[2048,128]{1,0:T(8,128)S(1)} custom-call(f32[2048,128]{1,0:T(8,128)} %bitcast.4, f32[1,64]{1,0:T(1,128)} %bitcast.5, f32[2,64]{1,0:T(2,128)} %wind_ref.1), custom_call_target="tpu_custom_call" | custom-call | tf_op jit(solution)/shard_map/parareal/pallas_call | solution.py:442
  22.2 1.0 %copy.5 = f32[1,64,32,128]{3,2,1,0:T(8,128)} copy(f32[1,64,32,128]{3,2,1,0:T(8,128)S(1)} %bitcast.3) | data formatting | bytes 2097152

commit v8 on v7

--- a/solution.py
+++ b/solution.py
@@ -185,8 +185,16 @@
     y_moves = tuple(m for m in AROUND if m[1] != 0)
     low_lanes = lane < levels
     high_lanes = lane >= LANES - levels
+    pl.semaphore_wait(barrier, awaited)
+
+    @pl.when(tm > 0)
+    def _():
+        pl.semaphore_signal(ready, inc=1, device_id=target(-1, 0, 0), device_id_type=pl.DeviceIdType.MESH)
+
+    send_all(fine_copies, 0, x_moves)
     for row in range(REACH, REACH + part):
         bring_in(row)
+    send_all(fine_copies, 0, y_moves)
 
     def restricted(source, row):
         total = source[REACH + row * RATIO, pl.ds(FRONT, cols), :]
@@ -217,14 +225,6 @@
     for row in range(part_c):
         old_wide[COARSE_REACH + row, pl.ds(FRONT, cols_c), :] = restricted(first, row)
     pack_strips(old_row, old_strips)
-    pl.semaphore_wait(barrier, awaited)
-
-    @pl.when(tm > 0)
-    def _():
-        pl.semaphore_signal(ready, inc=1, device_id=target(-1, 0, 0), device_id_type=pl.DeviceIdType.MESH)
-
-    send_all(fine_copies, 0, y_moves)
-    send_all(fine_copies, 0, x_moves)
     send_all(old_copies, 0, AROUND)
 
     def inside_x(row, reach, length):

time: 23.3 us -> 23.3 us (level)
  no operation moved by 1% of the time
where the time goes in v8:
time: 23.3 us; the launch traced here: 23.1 us
  Pallas kernels  22.1 us (95%)
  local copies, waits for them, and re-layouts  0.97 us (4%)
    pallas_call x1, Pallas kernels, shards(): pl.pallas_call(functools.partial(kernel, sizes, levels, rows, cols), out_...  22.1 us
    unnamed x1, local copies, waits for them, and re-layouts  0.97 us

profile of v8, /device:TPU:25, one launch (start us, length us, event | category | flops | bytes accessed | tf_op | source)
XLA Modules:
  0.0 23.1 jit_solution(994147148195005342)
XLA Ops:
  0.0 22.1 %parareal.1 = f32[2048,128]{1,0:T(8,128)S(1)} custom-call(f32[2048,128]{1,0:T(8,128)} %bitcast.4, f32[1,64]{1,0:T(1,128)} %bitcast.5, f32[2,64]{1,0:T(2,128)} %wind_ref.1), custom_call_target="tpu_custom_call" | custom-call | tf_op jit(solution)/shard_map/parareal/pallas_call | solution.py:442
  22.1 1.0 %copy.5 = f32[1,64,32,128]{3,2,1,0:T(8,128)} copy(f32[1,64,32,128]{3,2,1,0:T(8,128)S(1)} %bitcast.3) | data formatting | bytes 2097152
